TPU v7x, 512 devices: a whole 4x8x8 slice. The times are simulated.
512 devices in a mesh: space: 128 (over y, z, core), dp: 4 (over x).
Axes of the slice: x: 4, y: 8, z: 8, core: 2. Of those that a mesh axis runs over, the one named last changes fastest.
Arguments:
- features: bfloat16 [4, 65536, 128], P('dp', 'space'), may hold values from -6 to 6
- occupancy: int32 [4, 65536], P('dp', 'space'), may hold values from 0 to 1
- brick_pairs: int32 [4, 1024, 27], P('dp', 'space'), may hold values from 0 to 264, as said below
- send_lists: int32 [4, 128, 256], P('dp', 'space'), may hold values from -1 to 7, as said below
- scan_weight: int32 [4], P('dp'), may hold values from 1 to 12
- kernel: bfloat16 [3456, 128], replicated, may hold values from -0.109375 to 0.109375
- cotangent: bfloat16 [4, 65536, 128], P('dp', 'space'), may hold values from -6 to 6
Outputs:
- output_features: bfloat16 [4, 65536, 128], P('dp', 'space')
- grad_features: bfloat16 [4, 65536, 128], P('dp', 'space')
- grad_kernel: float32 [3456, 128], replicated
Inputs may be any that keep to these rules, and one draw needn't show every extreme that they name: `brick_pairs`: entry 13 of brick b is b itself. A value under 8 is a brick of the same owner; 8 + t * 2 + k names entry k of what owner t sends to this owner, and then t differs from this owner's index on space in exactly one bit; 264 is an empty brick. `send_lists`: for a destination t that differs from the owner's index in exactly one bit, 2 distinct slots of the owner; for every other destination all -1.
All inputs are finite; a program needn't handle non-finite values.
Results may differ from a plain program's by a relative error of at most 0.0017.
Values may be sent and summed in bfloat16 or wider, within the bound.
No kernel may reach another device: no remote copies, remote signals or barrier semaphores. Data moves between devices by JAX's collectives and lax.ppermute only.
A program may use at most 64 MiB of HBM per device.

v0:
```python
import math

import jax
import jax.numpy as jnp
import numpy as np
from jax import lax
from jax.sharding import PartitionSpec as P


def swapped(value, axis, bit):
    mask = 2**bit
    pairs = [(source, source ^ mask) for source in range(lax.axis_size(axis))]
    return lax.ppermute(value, axis, pairs)


def patch_layout():
    offset_list = []
    inner_list = []
    for pos_x in range(6):
        for pos_y in range(6):
            for pos_z in range(6):
                offset_parts = []
                inner_parts = []
                for coordinate in (pos_x, pos_y, pos_z):
                    shifted = coordinate - 1
                    brick_step = shifted // 4
                    offset_parts.append(brick_step + 1)
                    inner_parts.append(shifted - 4 * brick_step)
                offset_list.append(9 * offset_parts[0] + 3 * offset_parts[1] + offset_parts[2])
                inner_list.append(16 * inner_parts[0] + 4 * inner_parts[1] + inner_parts[2])
    return (np.array(offset_list, np.int32), np.array(inner_list, np.int32))


def convolve(table_rows, table_index, grad_in, kernel, offset_map, inner_map):
    bricks = table_index.shape[0]
    channels = table_rows.shape[1]
    patch_rows = table_index[:, offset_map] * 64 + inner_map[None, :]
    patch_cube = jnp.take(table_rows, patch_rows.reshape(-1), axis=0).reshape(
        bricks, 6, 6, 6, channels
    )
    result = jnp.zeros((bricks * 64, channels), jnp.float32)
    patch_grad = jnp.zeros((bricks, 6, 6, 6, channels), jnp.float32)
    weight_grads = []
    for shift_x in range(3):
        pieces = []
        for tap_index in range(9):
            shift_y = tap_index // 3
            shift_z = tap_index % 3
            pieces.append(
                patch_cube[
                    :, shift_x : shift_x + 4, shift_y : shift_y + 4, shift_z : shift_z + 4, :
                ].reshape(bricks * 64, channels)
            )
        columns = jnp.concatenate(pieces, axis=1)
        kernel_rows = kernel[shift_x * 9 * channels : (shift_x + 1) * 9 * channels]
        result = result + jnp.dot(columns, kernel_rows, preferred_element_type=jnp.float32)
        weight_grads.append(jnp.dot(columns.T, grad_in, preferred_element_type=jnp.float32))
        for tap_index in range(9):
            shift_y = tap_index // 3
            shift_z = tap_index % 3
            tap_weight = kernel_rows[tap_index * channels : (tap_index + 1) * channels]
            tap_grad = jnp.dot(grad_in, tap_weight.T, preferred_element_type=jnp.float32)
            patch_grad = patch_grad.at[
                :, shift_x : shift_x + 4, shift_y : shift_y + 4, shift_z : shift_z + 4, :
            ].add(tap_grad.reshape(bricks, 4, 4, 4, channels))
    table_grad = jax.ops.segment_sum(
        patch_grad.reshape(-1, channels), patch_rows.reshape(-1), num_segments=table_rows.shape[0]
    )
    return (result, table_grad, jnp.concatenate(weight_grads, axis=0))


def halo_index(pair_table, device, bricks, nspace, peer_cap, levels):
    zero_full = bricks + nspace * peer_cap
    relative = jnp.clip(pair_table - bricks, 0, nspace * peer_cap - 1)
    source = relative // peer_cap
    within = relative % peer_cap
    flipped = jnp.bitwise_xor(source, device)
    level_of = jnp.zeros_like(pair_table)
    for bit_level in range(levels):
        level_of = level_of + bit_level * (flipped == 1 << bit_level).astype(jnp.int32)
    compact = bricks + level_of * peer_cap + within
    outside = bricks + levels * peer_cap
    return jnp.where(
        pair_table < bricks, pair_table, jnp.where(pair_table >= zero_full, outside, compact)
    )


def pick_bricks(brick_rows, chosen):
    gathered = jnp.take(brick_rows, jnp.maximum(chosen, 0), axis=0)
    return jnp.where((chosen >= 0)[:, None], gathered, jnp.zeros_like(gathered))


def on_device(features, occupancy, brick_pairs, send_lists, scan_weight, kernel, cotangent):
    offset_list, inner_list = patch_layout()
    offset_map = jnp.asarray(offset_list, jnp.int32)
    inner_map = jnp.asarray(inner_list, jnp.int32)
    channels = features.shape[2]
    own_rows = features.shape[1]
    bricks = own_rows // 64
    nspace = lax.axis_size("space")
    scan_count = lax.axis_size("dp")
    levels = nspace.bit_length() - 1
    device = lax.axis_index("space")
    send_table = send_lists[0, 0]
    peer_cap = send_table.shape[0] // nspace
    voxel_mask = occupancy[0][:, None].astype(jnp.bfloat16)
    masked = features[0] * voxel_mask
    grad_in = cotangent[0] * voxel_mask
    brick_rows = masked.reshape(bricks, 64 * channels)
    empty_brick = jnp.zeros((1, 64 * channels), jnp.bfloat16)
    pair_table = brick_pairs[0]
    incoming = []
    for bit_level in range(levels):
        partner = jnp.bitwise_xor(device, 1 << bit_level)
        chosen = lax.dynamic_slice(send_table, (partner * peer_cap,), (peer_cap,))
        incoming.append(swapped(pick_bricks(brick_rows, chosen), "space", bit_level))
    brick_table = jnp.concatenate([brick_rows] + incoming + [empty_brick], axis=0).reshape(
        -1, channels
    )
    table_index = halo_index(pair_table, device, bricks, nspace, peer_cap, levels)
    result, table_grad, weight_grad = convolve(
        brick_table, table_index, grad_in, kernel, offset_map, inner_map
    )
    returned = jnp.zeros((bricks + 1, 64 * channels), jnp.float32)
    for bit_level in range(levels):
        partner = jnp.bitwise_xor(device, 1 << bit_level)
        chosen = lax.dynamic_slice(send_table, (partner * peer_cap,), (peer_cap,))
        start_row = own_rows + bit_level * peer_cap * 64
        grad_piece = (
            table_grad[start_row : start_row + peer_cap * 64]
            .astype(jnp.bfloat16)
            .reshape(peer_cap, 64 * channels)
        )
        came_back = swapped(grad_piece, "space", bit_level)
        target = jnp.where(chosen >= 0, chosen, bricks)
        returned = returned + jax.ops.segment_sum(
            came_back.astype(jnp.float32), target, num_segments=bricks + 1
        )
    returned = returned[:bricks]
    grad_sum = (
        grad_in.astype(jnp.float32) + table_grad[:own_rows] + returned.reshape(own_rows, channels)
    )
    own_weight = scan_weight[0].astype(jnp.float32)
    weighted = weight_grad * own_weight
    partial_sum, weight_total = lax.psum((weighted, own_weight), "dp")
    summed = lax.psum(partial_sum, "space")
    factor = own_weight * scan_count / weight_total
    mask_float = voxel_mask.astype(jnp.float32)
    output = (mask_float * (result + masked.astype(jnp.float32))).astype(jnp.bfloat16)
    grad_features = (factor * (mask_float * grad_sum)).astype(jnp.bfloat16)
    kernel_grad = summed * (scan_count / weight_total) / math.sqrt(64.0 * bricks * nspace)
    return (output[None], grad_features[None], kernel_grad)


def solution(mesh):
    return jax.shard_map(
        on_device,
        mesh=mesh,
        in_specs=(
            P("dp", "space", None),
            P("dp", "space"),
            P("dp", "space", None),
            P("dp", "space", None),
            P("dp"),
            P(),
            P("dp", "space", None),
        ),
        out_specs=(P("dp", "space", None), P("dp", "space", None), P()),
        check_vma=False,
    )
```

profile of v0, /device:TPU:1, one launch (start us, length us, event | category | flops | bytes accessed | tf_op | source)
XLA Modules:
  0.0 353.3 jit_solution(18334102057743575404)
XLA Ops:
  11.9 8.7 %collective-permute-start = (bf16[2,8192]{1,0:T(2,128)(2,1)S(1)}, bf16[2,8192]{1,0:T(2,128)(2,1)S(1)}, u32[]{:S(2)}, u32[]{:S(2)}) collective-permute-start(bf16[2,8192]{1,0:T(2,128)(2,1)S(1)} %broadcast_select_fusion.14), channel_id=1, source_target_pairs={{0,4},{4,0},{8,12},{12,8},{16,20},{20,16},{24,28},{28,24},{32,36},... | collective-permute-start | bytes 98312 | tf_op jit(solution)/shard_map/ppermute | solution.py:13
  21.4 1.9 collective-permute-start.1
  24.1 2.7 collective-permute-start.2
  27.5 7.9 %collective-permute-start.3 = (bf16[2,8192]{1,0:T(2,128)(2,1)S(1)}, bf16[2,8192]{1,0:T(2,128)(2,1)S(1)}, u32[]{:S(2)}, u32[]{:S(2)}) collective-permute-start(bf16[2,8192]{1,0:T(2,128)(2,1)S(1)} %broadcast_select_fusion.11), channel_id=1, source_target_pairs={{0,32},{4,36},{8,40},{12,44},{16,48},{20,52},{24,56},{28,60},{32,0... | collective-permute-start | bytes 98312 | tf_op jit(solution)/shard_map/ppermute | solution.py:13
  36.2 3.2 collective-permute-start.4
  44.0 2.1 fusion.21
  50.1 4.2 %collective-permute-start.5 = (bf16[2,8192]{1,0:T(2,128)(2,1)S(1)}, bf16[2,8192]{1,0:T(2,128)(2,1)S(1)}, u32[]{:S(2)}, u32[]{:S(2)}) collective-permute-start(bf16[2,8192]{1,0:T(2,128)(2,1)S(1)} %broadcast_select_fusion.9), channel_id=1, source_target_pairs={{0,128},{4,132},{8,136},{12,140},{16,144},{20,148},{24,152},{28,15... | collective-permute-start | bytes 98312 | tf_op jit(solution)/shard_map/ppermute | solution.py:13
  54.4 4.8 %collective-permute-start.6 = (bf16[2,8192]{1,0:T(2,128)(2,1)S(1)}, bf16[2,8192]{1,0:T(2,128)(2,1)S(1)}, u32[]{:S(2)}, u32[]{:S(2)}) collective-permute-start(bf16[2,8192]{1,0:T(2,128)(2,1)S(1)} %broadcast_select_fusion.8), channel_id=1, source_target_pairs={{0,256},{4,260},{8,264},{12,268},{16,272},{20,276},{24,280},{28,28... | collective-permute-start | bytes 98312 | tf_op jit(solution)/shard_map/ppermute | solution.py:13
  59.9 3.1 collective-permute-done.6
  63.8 3.9 %gather_fusion.1 = bf16[1728,128]{1,0:T(8,128)(2,1)S(1)} fusion(bf16[1472,128]{1,0:T(8,128)(2,1)S(1)} %reshape.1812, s32[2048]{0:T(1024)S(1)} %pad_clamp_fusion), kind=kCustom, calls=%fused_computation.8 | custom fusion | bytes 891648 | tf_op jit(solution)/shard_map/jit(_take)/gather | solution.py:38
  81.2 2.3 reshape.1928
  83.6 12.1 %scatter_custom_fusion = f32[1472,128]{1,0:T(8,128)S(1)} fusion(s32[1728]{0:T(1024)S(1)} %reshape.1926, f32[1728,128]{1,0:T(8,128)} %reshape.1928, f32[]{:T(128)} %constant.997.clone.1), kind=kCustom, calls=%fused_computation.75 | custom fusion | flops 221184 | bytes 754176 | tf_op jit(solution)/shard_map/scatter-add | solution.py:66
  98.3 2.1 collective-permute-start.9
  101.1 2.2 collective-permute-start.8
  103.8 4.9 %collective-permute-start.7 = (bf16[2,8192]{1,0:T(2,128)(2,1)}, bf16[2,8192]{1,0:T(2,128)(2,1)S(1)}, u32[]{:S(2)}, u32[]{:S(2)}) collective-permute-start(bf16[2,8192]{1,0:T(2,128)(2,1)} %reshape.1844), channel_id=1, source_target_pairs={{0,4},{4,0},{8,12},{12,8},{16,20},{20,16},{24,28},{28,24},{32,36},... | collective-permute-start | bytes 98312 | tf_op jit(solution)/shard_map/ppermute | solution.py:13
  109.4 2.4 collective-permute-start.11
  113.1 5.7 %collective-permute-start.13 = (bf16[2,8192]{1,0:T(2,128)(2,1)S(1)}, bf16[2,8192]{1,0:T(2,128)(2,1)S(1)}, u32[]{:S(2)}, u32[]{:S(2)}) collective-permute-start(bf16[2,8192]{1,0:T(2,128)(2,1)S(1)} %reshape.1850), channel_id=1, source_target_pairs={{0,256},{4,260},{8,264},{12,268},{16,272},{20,276},{24,280},{28,28... | collective-permute-start | bytes 98312 | tf_op jit(solution)/shard_map/ppermute | solution.py:13
  118.8 3.7 %collective-permute-start.12 = (bf16[2,8192]{1,0:T(2,128)(2,1)S(1)}, bf16[2,8192]{1,0:T(2,128)(2,1)}, u32[]{:S(2)}, u32[]{:S(2)}) collective-permute-start(bf16[2,8192]{1,0:T(2,128)(2,1)S(1)} %reshape.1849), channel_id=1, source_target_pairs={{0,128},{4,132},{8,136},{12,140},{16,144},{20,148},{24,152},{28,15... | collective-permute-start | bytes 98312 | tf_op jit(solution)/shard_map/ppermute | solution.py:13
  123.7 10.6 %psum.21 = f32[]{:T(128)} all-reduce(f32[]{:T(128)} %bitcast.46), channel_id=1, replica_groups=mesh['space'=128,'dp'=4] {'dp'}, use_global_device_ids=true, to_apply=%region_0.0 | all-reduce | flops 1 | bytes 8 | tf_op jit(solution)/shard_map/psum | solution.py:145
  137.1 1.9 scatter_custom_fusion.1
  139.0 2.0 add.424
  141.1 2.8 scatter_custom_fusion.3
  151.4 192.3 %all-reduce.6.cloned.1.call-done = f32[3456,128]{1,0:T(8,128)} async-done(((f32[3456,128]{1,0:T(8,128)}), f32[3456,128]{1,0:T(8,128)}) %all-reduce.6.cloned.1.call-update) | async-done | bytes 1769488 | tf_op jit(solution)/shard_map/psum | solution.py:146
  343.7 2.8 multiply_multiply_fusion
  (173 shorter events, 45.9 us)
Async XLA Ops:
  7.2 139.4 %all-reduce.4.cloned.1.call-start = ((), (), s32[]{:S(2)}) async-start(), calls=%async_computation | async-start | bytes 3538944 | tf_op jit(solution)/shard_map/psum | solution.py:145
  11.2 29.5 %copy-start.8 = (s32[1,8,27]{2,1,0:T(8,128)S(1)}, s32[1,8,27]{2,1,0:T(8,128)}, u32[]{:S(2)}) copy-start(s32[1,8,27]{2,1,0:T(8,128)} %param.67) | copy-start | bytes 2596
  11.8 29.0 %copy-start.10 = (s32[216]{0:T(256)S(1)}, s32[216]{0:T(256)}, u32[]{:S(2)}) copy-start(s32[216]{0:T(256)} %constant.1014) | copy-start | bytes 2596
  11.9 38.2 %collective-permute-start = (bf16[2,8192]{1,0:T(2,128)(2,1)S(1)}, bf16[2,8192]{1,0:T(2,128)(2,1)S(1)}, u32[]{:S(2)}, u32[]{:S(2)}) collective-permute-start(bf16[2,8192]{1,0:T(2,128)(2,1)S(1)} %broadcast_select_fusion.14), channel_id=1, source_target_pairs={{0,4},{4,0},{8,12},{12,8},{16,20},{20,16},{24,28},{28,24},{32,36},... | collective-permute-start | bytes 98312 | tf_op jit(solution)/shard_map/ppermute | solution.py:13
  20.7 20.9 %copy-start.9 = (s32[216]{0:T(256)S(1)}, s32[216]{0:T(256)}, u32[]{:S(2)}) copy-start(s32[216]{0:T(256)} %constant.1000.clone) | copy-start | bytes 2596
  21.3 20.8 %copy-start = (bf16[1,512,128]{2,1,0:T(8,128)(2,1)S(1)}, bf16[1,512,128]{2,1,0:T(8,128)(2,1)}, u32[]{:S(2)}) copy-start(bf16[1,512,128]{2,1,0:T(8,128)(2,1)} %param.71) | copy-start | bytes 393220
  21.4 32.9 %collective-permute-start.1 = (bf16[2,8192]{1,0:T(2,128)(2,1)S(1)}, bf16[2,8192]{1,0:T(2,128)(2,1)S(1)}, u32[]{:S(2)}, u32[]{:S(2)}) collective-permute-start(bf16[2,8192]{1,0:T(2,128)(2,1)S(1)} %broadcast_select_fusion.13), channel_id=1, source_target_pairs={{0,8},{4,12},{8,0},{12,4},{16,24},{20,28},{24,16},{28,20},{32,40},... | collective-permute-start | bytes 98312 | tf_op jit(solution)/shard_map/ppermute | solution.py:13
  24.0 18.2 %copy-start.1 = (bf16[3456,128]{1,0:T(8,128)(2,1)S(1)}, bf16[3456,128]{1,0:T(8,128)(2,1)}, u32[]{:S(2)}) copy-start(bf16[3456,128]{1,0:T(8,128)(2,1)} %param.70) | copy-start | bytes 2654212
  24.1 35.8 %collective-permute-start.2 = (bf16[2,8192]{1,0:T(2,128)(2,1)S(1)}, bf16[2,8192]{1,0:T(2,128)(2,1)S(1)}, u32[]{:S(2)}, u32[]{:S(2)}) collective-permute-start(bf16[2,8192]{1,0:T(2,128)(2,1)S(1)} %broadcast_select_fusion.12), channel_id=1, source_target_pairs={{0,16},{4,20},{8,24},{12,28},{16,0},{20,4},{24,8},{28,12},{32,48},... | collective-permute-start | bytes 98312 | tf_op jit(solution)/shard_map/ppermute | solution.py:13
  27.5 32.4 %collective-permute-start.3 = (bf16[2,8192]{1,0:T(2,128)(2,1)S(1)}, bf16[2,8192]{1,0:T(2,128)(2,1)S(1)}, u32[]{:S(2)}, u32[]{:S(2)}) collective-permute-start(bf16[2,8192]{1,0:T(2,128)(2,1)S(1)} %broadcast_select_fusion.11), channel_id=1, source_target_pairs={{0,32},{4,36},{8,40},{12,44},{16,48},{20,52},{24,56},{28,60},{32,0... | collective-permute-start | bytes 98312 | tf_op jit(solution)/shard_map/ppermute | solution.py:13
  36.2 23.8 %collective-permute-start.4 = (bf16[2,8192]{1,0:T(2,128)(2,1)S(1)}, bf16[2,8192]{1,0:T(2,128)(2,1)S(1)}, u32[]{:S(2)}, u32[]{:S(2)}) collective-permute-start(bf16[2,8192]{1,0:T(2,128)(2,1)S(1)} %broadcast_select_fusion.10), channel_id=1, source_target_pairs={{0,64},{4,68},{8,72},{12,76},{16,80},{20,84},{24,88},{28,92},{32,9... | collective-permute-start | bytes 98312 | tf_op jit(solution)/shard_map/ppermute | solution.py:13
  50.1 9.8 %collective-permute-start.5 = (bf16[2,8192]{1,0:T(2,128)(2,1)S(1)}, bf16[2,8192]{1,0:T(2,128)(2,1)S(1)}, u32[]{:S(2)}, u32[]{:S(2)}) collective-permute-start(bf16[2,8192]{1,0:T(2,128)(2,1)S(1)} %broadcast_select_fusion.9), channel_id=1, source_target_pairs={{0,128},{4,132},{8,136},{12,140},{16,144},{20,148},{24,152},{28,15... | collective-permute-start | bytes 98312 | tf_op jit(solution)/shard_map/ppermute | solution.py:13
  54.4 8.7 %collective-permute-start.6 = (bf16[2,8192]{1,0:T(2,128)(2,1)S(1)}, bf16[2,8192]{1,0:T(2,128)(2,1)S(1)}, u32[]{:S(2)}, u32[]{:S(2)}) collective-permute-start(bf16[2,8192]{1,0:T(2,128)(2,1)S(1)} %broadcast_select_fusion.8), channel_id=1, source_target_pairs={{0,256},{4,260},{8,264},{12,268},{16,272},{20,276},{24,280},{28,28... | collective-permute-start | bytes 98312 | tf_op jit(solution)/shard_map/ppermute | solution.py:13
  74.9 268.8 %all-reduce.6.cloned.1.call-start = ((), (), s32[]{:S(2)}) async-start(), calls=%async_computation.1 | async-start | bytes 3538944 | tf_op jit(solution)/shard_map/psum | solution.py:146
  83.6 28.3 %copy-start.6 = (s32[1,1,256]{2,1,0:T(1,128)S(1)}, s32[1,1,256]{2,1,0:T(1,128)}, u32[]{:S(2)}) copy-start(s32[1,1,256]{2,1,0:T(1,128)} %param.68) | copy-start | bytes 3076
  96.4 16.8 %collective-permute-start.10 = (bf16[2,8192]{1,0:T(2,128)(2,1)}, bf16[2,8192]{1,0:T(2,128)(2,1)S(1)}, u32[]{:S(2)}, u32[]{:S(2)}) collective-permute-start(bf16[2,8192]{1,0:T(2,128)(2,1)} %reshape.1847), channel_id=1, source_target_pairs={{0,32},{4,36},{8,40},{12,44},{16,48},{20,52},{24,56},{28,60},{32,0... | collective-permute-start | bytes 98312 | tf_op jit(solution)/shard_map/ppermute | solution.py:13
  98.3 38.8 %collective-permute-start.9 = (bf16[2,8192]{1,0:T(2,128)(2,1)S(1)}, bf16[2,8192]{1,0:T(2,128)(2,1)S(1)}, u32[]{:S(2)}, u32[]{:S(2)}) collective-permute-start(bf16[2,8192]{1,0:T(2,128)(2,1)S(1)} %reshape.1846), channel_id=1, source_target_pairs={{0,16},{4,20},{8,24},{12,28},{16,0},{20,4},{24,8},{28,12},{32,48},... | collective-permute-start | bytes 98312 | tf_op jit(solution)/shard_map/ppermute | solution.py:13
  101.1 36.0 %collective-permute-start.8 = (bf16[2,8192]{1,0:T(2,128)(2,1)}, bf16[2,8192]{1,0:T(2,128)(2,1)S(1)}, u32[]{:S(2)}, u32[]{:S(2)}) collective-permute-start(bf16[2,8192]{1,0:T(2,128)(2,1)} %reshape.1845), channel_id=1, source_target_pairs={{0,8},{4,12},{8,0},{12,4},{16,24},{20,28},{24,16},{28,20},{32,40},... | collective-permute-start | bytes 98312 | tf_op jit(solution)/shard_map/ppermute | solution.py:13
  103.8 33.2 %collective-permute-start.7 = (bf16[2,8192]{1,0:T(2,128)(2,1)}, bf16[2,8192]{1,0:T(2,128)(2,1)S(1)}, u32[]{:S(2)}, u32[]{:S(2)}) collective-permute-start(bf16[2,8192]{1,0:T(2,128)(2,1)} %reshape.1844), channel_id=1, source_target_pairs={{0,4},{4,0},{8,12},{12,8},{16,20},{20,16},{24,28},{28,24},{32,36},... | collective-permute-start | bytes 98312 | tf_op jit(solution)/shard_map/ppermute | solution.py:13
  109.4 9.4 %collective-permute-start.11 = (bf16[2,8192]{1,0:T(2,128)(2,1)}, bf16[2,8192]{1,0:T(2,128)(2,1)S(1)}, u32[]{:S(2)}, u32[]{:S(2)}) collective-permute-start(bf16[2,8192]{1,0:T(2,128)(2,1)} %reshape.1848), channel_id=1, source_target_pairs={{0,64},{4,68},{8,72},{12,76},{16,80},{20,84},{24,88},{28,92},{32,9... | collective-permute-start | bytes 98312 | tf_op jit(solution)/shard_map/ppermute | solution.py:13
  113.1 27.9 %collective-permute-start.13 = (bf16[2,8192]{1,0:T(2,128)(2,1)S(1)}, bf16[2,8192]{1,0:T(2,128)(2,1)S(1)}, u32[]{:S(2)}, u32[]{:S(2)}) collective-permute-start(bf16[2,8192]{1,0:T(2,128)(2,1)S(1)} %reshape.1850), channel_id=1, source_target_pairs={{0,256},{4,260},{8,264},{12,268},{16,272},{20,276},{24,280},{28,28... | collective-permute-start | bytes 98312 | tf_op jit(solution)/shard_map/ppermute | solution.py:13
  118.8 22.2 %collective-permute-start.12 = (bf16[2,8192]{1,0:T(2,128)(2,1)S(1)}, bf16[2,8192]{1,0:T(2,128)(2,1)}, u32[]{:S(2)}, u32[]{:S(2)}) collective-permute-start(bf16[2,8192]{1,0:T(2,128)(2,1)S(1)} %reshape.1849), channel_id=1, source_target_pairs={{0,128},{4,132},{8,136},{12,140},{16,144},{20,148},{24,152},{28,15... | collective-permute-start | bytes 98312 | tf_op jit(solution)/shard_map/ppermute | solution.py:13
  146.6 1.5 copy-start.2
  148.1 1.3 copy-start.4
  (3 other events, 3.0 us)
Sparse Core Ops, SparseCore 0:
  75.0 59.4 all-reduce.3
  146.7 196.9 all-reduce.5
where the time goes:
time: 356 us; the launch traced here: 353 us
  waiting for transfers between devices  195 us (55%)
  starting transfers between devices  56.6 us (16%)
  other arithmetic  32.3 us (9%)
  local copies, waits for them, and re-layouts  24.9 us (7%)
  between operations  17 us (5%)
  matrix products  16.5 us (5%)
  blocking collectives  10.6 us (3%)
    psum x1, waiting for transfers between devices, on_device(): summed = lax.psum(partial_sum, 'space')  192 us
    ppermute x14, starting transfers between devices, swapped(): return lax.ppermute(value, axis, pairs)  56.3 us
    scatter-add x1, other arithmetic, convolve(): jax.ops.segment_sum(patch_grad.reshape(-1, channels), patch_rows.reshape(...  12.1 us
    dot_general x27, matrix products, convolve(): jnp.dot(grad_in, tap_weight.T, preferred_element_type=jnp.float32)  11.6 us
    psum x1, blocking collectives, on_device(): partial_sum, weight_total = lax.psum((weighted, own_weight), 'dp')  10.6 us
  transfers between devices with their start and end apart: 16, of which 2 were waited for; matrix products, arithmetic and copies ran while one was open for 15% of the time, Pallas kernels for 0%

commit v1 on v0

v1 whole, which is shorter than its diff:
```python
import math

import jax
import jax.numpy as jnp
import numpy as np
from jax import lax
from jax.sharding import Mesh, PartitionSpec as P


SPACE = ("y", "z", "core")
FULL = 16383.0
FULL_BITS = 14
SHARD_ROWS = 64
SPARE = 16


def bit_axes(sizes):
    steps = []
    for axis in reversed(SPACE):
        for bit in range(sizes[axis].bit_length() - 1):
            steps.append((axis, bit))
    return steps


def swapped(value, step):
    axis, bit = step
    pairs = [(source, source ^ 2**bit) for source in range(lax.axis_size(axis))]
    return lax.ppermute(value, axis, pairs)


def encode(values, extra=None):
    rows = values.shape[-2]
    peak = jnp.max(jnp.abs(values), axis=-2, keepdims=True)
    power = jnp.clip(jnp.ceil(jnp.log2(jnp.maximum(peak, 1e-30))), -100.0, 100.0)
    coded = jnp.round(values * jnp.exp2(FULL_BITS - power)).astype(jnp.int16)
    spare = [power.astype(jnp.int16)]
    if extra is not None:
        spare.append(jnp.broadcast_to(extra.astype(jnp.int16), power.shape))
    fill = -rows % SPARE or SPARE
    spare.append(jnp.zeros(values.shape[:-2] + (fill - len(spare), values.shape[-1]), jnp.int16))
    return jnp.concatenate([coded] + spare, axis=-2)


def decode(coded, rows):
    power = coded[..., rows : rows + 1, :].astype(jnp.float32)
    return coded[..., :rows, :].astype(jnp.float32) * jnp.exp2(power - FULL_BITS)


def exchanged(parts, axes):
    return lax.all_to_all(parts, axes, 0, 0, tiled=True)


def everyone(part, axes, count):
    return exchanged(jnp.broadcast_to(part[None], (count,) + part.shape), axes)


def reduced(weighted, own_weight):
    rows, channels = weighted.shape
    near = ("core", "x")
    near_count = lax.axis_size("core") * lax.axis_size("x")
    depth = lax.axis_size("z")
    breadth = lax.axis_size("y")
    near_rows = rows // near_count
    own_rows = near_rows // depth
    parts = exchanged(encode(weighted.reshape(near_count, near_rows, channels), own_weight), near)
    total_weight = jnp.sum(parts[:, near_rows + 1, 0].astype(jnp.float32)) / lax.axis_size("core")
    part = jnp.sum(decode(parts, near_rows), axis=0)
    parts = exchanged(encode(part.reshape(depth, own_rows, channels)), "z")
    part = jnp.sum(decode(parts, own_rows), axis=0)
    parts = everyone(encode(part), "y", breadth)
    part = jnp.sum(decode(parts, own_rows), axis=0)
    part = decode(everyone(encode(part), "z", depth), own_rows).reshape(near_rows, channels)
    whole = decode(everyone(encode(part), near, near_count), near_rows).reshape(rows, channels)
    return whole, total_weight


def patch_layout():
    offset_list = []
    inner_list = []
    for pos_x in range(6):
        for pos_y in range(6):
            for pos_z in range(6):
                offset_parts = []
                inner_parts = []
                for coordinate in (pos_x, pos_y, pos_z):
                    shifted = coordinate - 1
                    brick_step = shifted // 4
                    offset_parts.append(brick_step + 1)
                    inner_parts.append(shifted - 4 * brick_step)
                offset_list.append(9 * offset_parts[0] + 3 * offset_parts[1] + offset_parts[2])
                inner_list.append(16 * inner_parts[0] + 4 * inner_parts[1] + inner_parts[2])
    return (np.array(offset_list, np.int32), np.array(inner_list, np.int32))


def gradients(table_index, grad_in, kernel, offset_map, inner_map, table_rows):
    bricks = table_index.shape[0]
    channels = grad_in.shape[1]
    patch_rows = table_index[:, offset_map] * 64 + inner_map[None, :]
    patch_grad = jnp.zeros((bricks, 6, 6, 6, channels), jnp.float32)
    for tap in range(27):
        x, y, z = tap // 9, tap // 3 % 3, tap % 3
        tap_weight = kernel[tap * channels : (tap + 1) * channels]
        tap_grad = jnp.dot(grad_in, tap_weight.T, preferred_element_type=jnp.float32)
        patch_grad = patch_grad.at[:, x : x + 4, y : y + 4, z : z + 4, :].add(
            tap_grad.reshape(bricks, 4, 4, 4, channels)
        )
    return jax.ops.segment_sum(
        patch_grad.reshape(-1, channels), patch_rows.reshape(-1), num_segments=table_rows
    )


def convolve(table_rows, table_index, grad_in, kernel, offset_map, inner_map):
    bricks = table_index.shape[0]
    channels = table_rows.shape[1]
    patch_rows = table_index[:, offset_map] * 64 + inner_map[None, :]
    patch_cube = jnp.take(table_rows, patch_rows.reshape(-1), axis=0).reshape(
        bricks, 6, 6, 6, channels
    )
    result = jnp.zeros((bricks * 64, channels), jnp.float32)
    weight_grads = []
    for x in range(3):
        pieces = []
        for tap in range(9):
            y, z = tap // 3, tap % 3
            pieces.append(
                patch_cube[:, x : x + 4, y : y + 4, z : z + 4, :].reshape(bricks * 64, channels)
            )
        columns = jnp.concatenate(pieces, axis=1)
        kernel_rows = kernel[x * 9 * channels : (x + 1) * 9 * channels]
        result = result + jnp.dot(columns, kernel_rows, preferred_element_type=jnp.float32)
        weight_grads.append(jnp.dot(columns.T, grad_in, preferred_element_type=jnp.float32))
    return (result, jnp.concatenate(weight_grads, axis=0))


def halo_index(pair_table, device, bricks, nspace, peer_cap, levels):
    zero_full = bricks + nspace * peer_cap
    relative = jnp.clip(pair_table - bricks, 0, nspace * peer_cap - 1)
    source = relative // peer_cap
    within = relative % peer_cap
    flipped = jnp.bitwise_xor(source, device)
    level_of = jnp.zeros_like(pair_table)
    for bit_level in range(levels):
        level_of = level_of + bit_level * (flipped == 1 << bit_level).astype(jnp.int32)
    compact = bricks + level_of * peer_cap + within
    outside = bricks + levels * peer_cap
    return jnp.where(
        pair_table < bricks, pair_table, jnp.where(pair_table >= zero_full, outside, compact)
    )


def pick_bricks(brick_rows, chosen):
    gathered = jnp.take(brick_rows, jnp.maximum(chosen, 0), axis=0)
    return jnp.where((chosen >= 0)[:, None], gathered, jnp.zeros_like(gathered))


def on_device(features, occupancy, brick_pairs, send_lists, scan_weight, kernel, cotangent):
    offset_list, inner_list = patch_layout()
    offset_map = jnp.asarray(offset_list, jnp.int32)
    inner_map = jnp.asarray(inner_list, jnp.int32)
    channels = features.shape[2]
    own_rows = features.shape[1]
    bricks = own_rows // 64
    nspace = lax.axis_size(SPACE)
    scan_count = lax.axis_size("x")
    steps = bit_axes({axis: lax.axis_size(axis) for axis in SPACE})
    levels = len(steps)
    device = lax.axis_index(SPACE)
    send_table = send_lists[0, 0]
    peer_cap = send_table.shape[0] // nspace
    voxel_mask = occupancy[0][:, None].astype(jnp.bfloat16)
    masked = features[0] * voxel_mask
    grad_in = cotangent[0] * voxel_mask
    brick_rows = masked.reshape(bricks, 64 * channels)
    empty_brick = jnp.zeros((1, 64 * channels), jnp.bfloat16)
    pair_table = brick_pairs[0]
    table_index = halo_index(pair_table, device, bricks, nspace, peer_cap, levels)
    table_grad = gradients(table_index, grad_in, kernel, offset_map, inner_map, (bricks + levels * peer_cap + 1) * 64)
    incoming = []
    returned = jnp.zeros((bricks + 1, 64 * channels), jnp.float32)
    for bit_level in range(levels):
        partner = jnp.bitwise_xor(device, 1 << bit_level)
        chosen = lax.dynamic_slice(send_table, (partner * peer_cap,), (peer_cap,))
        start_row = own_rows + bit_level * peer_cap * 64
        grad_piece = (
            table_grad[start_row : start_row + peer_cap * 64]
            .astype(jnp.bfloat16)
            .reshape(peer_cap, 64 * channels)
        )
        sent = jnp.concatenate([pick_bricks(brick_rows, chosen), grad_piece], axis=0)
        came = swapped(sent, steps[bit_level])
        incoming.append(came[:peer_cap])
        target = jnp.where(chosen >= 0, chosen, bricks)
        returned = returned + jax.ops.segment_sum(
            came[peer_cap:].astype(jnp.float32), target, num_segments=bricks + 1
        )
    brick_table = jnp.concatenate([brick_rows] + incoming + [empty_brick], axis=0).reshape(
        -1, channels
    )
    result, weight_grad = convolve(
        brick_table, table_index, grad_in, kernel, offset_map, inner_map
    )
    returned = returned[:bricks]
    grad_sum = (
        grad_in.astype(jnp.float32) + table_grad[:own_rows] + returned.reshape(own_rows, channels)
    )
    own_weight = scan_weight[0].astype(jnp.float32)
    summed, weight_total = reduced(weight_grad * own_weight, own_weight)
    factor = own_weight * scan_count / weight_total
    mask_float = voxel_mask.astype(jnp.float32)
    output = (mask_float * (result + masked.astype(jnp.float32))).astype(jnp.bfloat16)
    grad_features = (factor * (mask_float * grad_sum)).astype(jnp.bfloat16)
    kernel_grad = summed * (scan_count / weight_total) / math.sqrt(64.0 * bricks * nspace)
    return (output[None], grad_features[None], kernel_grad)


def solution(mesh):
    sizes = dict(mesh.shape)
    assert mesh.axis_names == ("space", "dp")
    inner = Mesh(
        mesh.devices.reshape(8, sizes["space"] // 16, 2, sizes["dp"]), ("y", "z", "core", "x")
    )
    return jax.shard_map(
        on_device,
        mesh=inner,
        in_specs=(
            P("x", SPACE, None),
            P("x", SPACE),
            P("x", SPACE, None),
            P("x", SPACE, None),
            P("x"),
            P(),
            P("x", SPACE, None),
        ),
        out_specs=(P("x", SPACE, None), P("x", SPACE, None), P()),
        check_vma=False,
    )
```

time: 356 us -> 182 us (0.51)
  waiting for transfers between devices: 195 us -> 28.3 us
  between operations: 17 us -> 3.26 us
  other arithmetic: 32.3 us -> 38 us
  local copies, waits for them, and re-layouts: 24.9 us -> 28.5 us
    psum x2 -> x0, waiting for transfers between devices: 192 us -> none  [the longest x1 192 us: on_device(): summed = lax.psum(partial_sum, 'space')]
    all_to_all x0 -> x4, waiting for transfers between devices: none -> 26.3 us  [exchanged(): return lax.all_to_all(parts, axes, 0, 0, tiled=True)]
    ppermute x14 -> x7, starting transfers between devices: 56.3 us -> 33.5 us  [swapped(): return lax.ppermute(value, axis, pairs)]
    all_to_all x0 -> x4, starting transfers between devices: none -> 21.8 us  [exchanged(): return lax.all_to_all(parts, axes, 0, 0, tiled=True)]
    all_to_all x0 -> x1, blocking collectives: none -> 10.8 us  [exchanged(): return lax.all_to_all(parts, axes, 0, 0, tiled=True)]
    psum x1 -> x0, blocking collectives: 10.6 us -> none  [on_device(): partial_sum, weight_total = lax.psum((weighted, own_weight), 'dp')]
    slice x2 -> x14, local copies, waits for them, and re-layouts: 1.92 us -> 6.94 us  [the longest x6 2.74 us: on_device(): came[peer_cap:].astype(jnp.float32)]
    reduce_sum x0 -> x4, other arithmetic: none -> 4.56 us  [the longest x1 2.22 us: reduced(): part = jnp.sum(decode(parts, near_rows), axis=0)]
  transfers between devices with their start and end apart: 16 -> 11, of which waited for: 2 -> 4; matrix products, arithmetic and copies ran while one was open for 15% -> 15% of each run, Pallas kernels for 0% -> 0%
where the time goes in v1:
time: 182 us; the launch traced here: 180 us
  starting transfers between devices  55.3 us (30%)
  other arithmetic  38 us (21%)
  local copies, waits for them, and re-layouts  28.5 us (16%)
  waiting for transfers between devices  28.3 us (16%)
  matrix products  16.1 us (9%)
  blocking collectives  10.8 us (6%)
  between operations  3.26 us (2%)
    ppermute x7, starting transfers between devices, swapped(): return lax.ppermute(value, axis, pairs)  33.5 us
    all_to_all x4, waiting for transfers between devices, exchanged(): return lax.all_to_all(parts, axes, 0, 0, tiled=True)  26.3 us
    all_to_all x4, starting transfers between devices, exchanged(): return lax.all_to_all(parts, axes, 0, 0, tiled=True)  21.8 us
    scatter-add x1, other arithmetic, gradients(): jax.ops.segment_sum(patch_grad.reshape(-1, channels), patch_rows.reshape(...  11.8 us
    all_to_all x1, blocking collectives, exchanged(): return lax.all_to_all(parts, axes, 0, 0, tiled=True)  10.8 us
    dot_general x27, matrix products, gradients(): jnp.dot(grad_in, tap_weight.T, preferred_element_type=jnp.float32)  8.51 us
    add x3, other arithmetic, on_device(): returned + jax.ops.segment_sum(came[peer_cap:].astype(jnp.float32), targe...  6.5 us
    dot_general x3, matrix products, convolve(): jnp.dot(columns, kernel_rows, preferred_element_type=jnp.float32)  5.78 us
  transfers between devices with their start and end apart: 11, of which 4 were waited for; matrix products, arithmetic and copies ran while one was open for 15% of the time, Pallas kernels for 0%

profile of v1, /device:TPU:1, one launch (start us, length us, event | category | flops | bytes accessed | tf_op | source)
XLA Modules:
  0.0 180.4 jit_solution(13873544168541711830)
XLA Ops:
  11.5 2.1 %fusion.22 = f32[8,6,6,6,128]{4,0,3,2,1:T(8,128)S(1)} fusion(f32[8,6,6,6,128]{4,0,3,2,1:T(8,128)S(1)} %fusion.23, s32[]{:T(128)} %bitcast.16, s32[]{:T(128)} %bitcast.17, s32[]{:T(128)} %bitcast.18, bf16[8,4,4,4,128]{4,0,3,2,1:T(8,128)(2,1)S(1)} %copy_multiply_fusion, bf16[3456,128]{1,0:T(8,128)(2,1)S(1)} %copy-done.1), kind=kOutput, calls=%fused_computation.64 | convolution fusion | flops 16842752 | bytes 688140 | tf_op jit(solution)/shard_map/dot_general | solution.py:103
  18.8 11.8 %scatter_custom_fusion = f32[1472,128]{1,0:T(8,128)S(1)} fusion(s32[1728]{0:T(1024)S(1)} %reshape.2177, f32[1728,128]{1,0:T(8,128)S(1)} %reshape.2179, f32[]{:T(128)} %constant.1027.clone.1), kind=kCustom, calls=%fused_computation.79 | custom fusion | flops 221184 | bytes 753668 | tf_op jit(solution)/shard_map/scatter-add | solution.py:107
  31.6 8.7 %collective-permute-start = (bf16[4,8192]{1,0:T(4,128)(2,1)S(1)}, bf16[4,8192]{1,0:T(4,128)(2,1)S(1)}, u32[]{:S(2)}, u32[]{:S(2)}) collective-permute-start(bf16[4,8192]{1,0:T(4,128)(2,1)S(1)} %pad_maximum_fusion), channel_id=1, source_target_pairs={{0,4},{4,0},{1,5},{5,1},{2,6},{6,2},{3,7},{7,3},{8,12},{12,8},{9,1... | collective-permute-start | bytes 196616 | tf_op jit(solution)/shard_map/ppermute | solution.py:28
  41.2 1.9 %collective-permute-start.1 = (bf16[4,8192]{1,0:T(4,128)(2,1)S(1)}, bf16[4,8192]{1,0:T(4,128)(2,1)S(1)}, u32[]{:S(2)}, u32[]{:S(2)}) collective-permute-start(bf16[4,8192]{1,0:T(4,128)(2,1)S(1)} %pad_maximum_fusion.1), channel_id=1, source_target_pairs={{0,8},{8,0},{16,24},{24,16},{32,40},{40,32},{48,56},{56,48},{1,9},... | collective-permute-start | bytes 196616 | tf_op jit(solution)/shard_map/ppermute | solution.py:28
  43.9 2.5 %collective-permute-start.2 = (bf16[4,8192]{1,0:T(4,128)(2,1)S(1)}, bf16[4,8192]{1,0:T(4,128)(2,1)S(1)}, u32[]{:S(2)}, u32[]{:S(2)}) collective-permute-start(bf16[4,8192]{1,0:T(4,128)(2,1)S(1)} %pad_maximum_fusion.2), channel_id=1, source_target_pairs={{0,16},{8,24},{16,0},{24,8},{32,48},{40,56},{48,32},{56,40},{1,17}... | collective-permute-start | bytes 196616 | tf_op jit(solution)/shard_map/ppermute | solution.py:28
  47.3 7.9 %collective-permute-start.3 = (bf16[4,8192]{1,0:T(4,128)(2,1)S(1)}, bf16[4,8192]{1,0:T(4,128)(2,1)S(1)}, u32[]{:S(2)}, u32[]{:S(2)}) collective-permute-start(bf16[4,8192]{1,0:T(4,128)(2,1)S(1)} %pad_maximum_fusion.3), channel_id=1, source_target_pairs={{0,32},{8,40},{16,48},{24,56},{32,0},{40,8},{48,16},{56,24},{1,33}... | collective-permute-start | bytes 196616 | tf_op jit(solution)/shard_map/ppermute | solution.py:28
  56.1 3.2 %collective-permute-start.4 = (bf16[4,8192]{1,0:T(4,128)(2,1)S(1)}, bf16[4,8192]{1,0:T(4,128)(2,1)S(1)}, u32[]{:S(2)}, u32[]{:S(2)}) collective-permute-start(bf16[4,8192]{1,0:T(4,128)(2,1)S(1)} %pad_maximum_fusion.4), channel_id=1, source_target_pairs={{0,64},{64,0},{128,192},{192,128},{256,320},{320,256},{384,448},{4... | collective-permute-start | bytes 196616 | tf_op jit(solution)/shard_map/ppermute | solution.py:28
  62.1 4.2 %collective-permute-start.5 = (bf16[4,8192]{1,0:T(4,128)(2,1)S(1)}, bf16[4,8192]{1,0:T(4,128)(2,1)S(1)}, u32[]{:S(2)}, u32[]{:S(2)}) collective-permute-start(bf16[4,8192]{1,0:T(4,128)(2,1)S(1)} %pad_maximum_fusion.5), channel_id=1, source_target_pairs={{0,128},{64,192},{128,0},{192,64},{256,384},{320,448},{384,256},{4... | collective-permute-start | bytes 196616 | tf_op jit(solution)/shard_map/ppermute | solution.py:28
  66.4 4.9 %collective-permute-start.6 = (bf16[4,8192]{1,0:T(4,128)(2,1)S(1)}, bf16[4,8192]{1,0:T(4,128)(2,1)S(1)}, u32[]{:S(2)}, u32[]{:S(2)}) collective-permute-start(bf16[4,8192]{1,0:T(4,128)(2,1)S(1)} %pad_maximum_fusion.6), channel_id=1, source_target_pairs={{0,256},{64,320},{128,384},{192,448},{256,0},{320,64},{384,128},{4... | collective-permute-start | bytes 196616 | tf_op jit(solution)/shard_map/ppermute | solution.py:28
  73.4 2.0 %collective-permute-done.6 = bf16[4,8192]{1,0:T(4,128)(2,1)S(1)} collective-permute-done((bf16[4,8192]{1,0:T(4,128)(2,1)S(1)}, bf16[4,8192]{1,0:T(4,128)(2,1)S(1)}, u32[]{:S(2)}, u32[]{:S(2)}) %collective-permute-start.6) | collective-permute-done | bytes 65568 | tf_op jit(solution)/shard_map/ppermute | solution.py:28
  76.8 3.9 %gather_fusion.1 = bf16[1728,128]{1,0:T(8,128)(2,1)S(1)} fusion(bf16[1472,128]{1,0:T(8,128)(2,1)S(1)} %reshape.2052, s32[2048]{0:T(1024)S(1)} %pad_clamp_fusion), kind=kCustom, calls=%fused_computation.8 | custom fusion | bytes 891648 | tf_op jit(solution)/shard_map/jit(_take)/gather | solution.py:116
  89.0 7.1 %all-to-all-start = ((s16[8,448,128]{2,1,0:T(8,128)(2,1)}), s16[8,448,128]{2,1,0:T(8,128)(2,1)}, u32[]{:S(2)}, u32[]{:S(2)}) async-start(s16[8,448,128]{2,1,0:T(8,128)(2,1)} %add_add_fusion), calls=%async_computation | async-start | bytes 1835008 | tf_op jit(solution)/shard_map/all_to_all | solution.py:50
  96.2 13.6 %all-to-all-done = s16[8,448,128]{2,1,0:T(8,128)(2,1)} async-done(((s16[8,448,128]{2,1,0:T(8,128)(2,1)}), s16[8,448,128]{2,1,0:T(8,128)(2,1)}, u32[]{:S(2)}, u32[]{:S(2)}) %all-to-all-start) | async-done | bytes 917536 | tf_op jit(solution)/shard_map/all_to_all | solution.py:50
  110.5 2.2 %multiply_reduce_fusion = f32[432,128]{1,0:T(8,128)} fusion(s16[8,448,128]{2,1,0:T(8,128)(2,1)} %all-to-all-done, f32[8,128]{1,0:T(8,128)S(1)} %exponential_bitcast_fusion.4), kind=kLoop, calls=%fused_computation.15 | loop fusion | flops 1271808 | bytes 1110016 | tf_op jit(solution)/shard_map/reduce_sum | solution.py:67
  113.9 10.8 %all_to_all.25 = s16[8,64,128]{2,1,0:T(8,128)(2,1)S(1)} all-to-all(s16[8,64,128]{2,1,0:T(8,128)(2,1)S(1)} %add_add_fusion.1), channel_id=1, replica_groups=mesh['y'=8,'z'=8,'core'=2,'x'=4] {'z'}, dimensions={0} | all-to-all | bytes 262144 | tf_op jit(solution)/shard_map/all_to_all | solution.py:50
  125.6 4.3 %all-to-all-start.2 = ((s16[8,64,128]{2,1,0:T(8,128)(2,1)}), s16[8,64,128]{2,1,0:T(8,128)(2,1)}, u32[]{:S(2)}, u32[]{:S(2)}) async-start(s16[8,64,128]{2,1,0:T(8,128)(2,1)} %broadcast_in_dim.158), calls=%async_computation.2 | async-start | bytes 262144 | tf_op jit(solution)/shard_map/all_to_all | solution.py:50
  133.9 2.1 %add.425 = f32[9,8192]{1,0:T(8,128)} add(f32[9,8192]{1,0:T(8,128)} %scatter_custom_fusion.1, f32[9,8192]{1,0:T(8,128)} %scatter_custom_fusion.2) | non-fusion elementwise | flops 73728 | bytes 884736 | tf_op jit(solution)/shard_map/add | solution.py:193
  136.0 2.6 %scatter_custom_fusion.3 = f32[9,8192]{1,0:T(8,128)} fusion(f32[9,8192]{1,0:T(8,128)} %add.425, s32[4]{0:T(128)S(1)} %add_bitcast_fusion.1, bf16[2,8192]{1,0:T(2,128)(2,1)S(1)} %copy-done.9, bf16[]{:T(256)} %constant.1065, bf16[2,8192]{1,0:T(2,128)(2,1)S(1)} %copy-done.8), kind=kCustom, calls=%fused_computation.116 | custom fusion | flops 163840 | bytes 360960 | tf_op jit(solution)/shard_map/add | solution.py:193
  143.8 4.0 %all-to-all-start.3 = ((s16[8,64,128]{2,1,0:T(8,128)(2,1)}), s16[8,64,128]{2,1,0:T(8,128)(2,1)}, u32[]{:S(2)}, u32[]{:S(2)}) async-start(s16[8,64,128]{2,1,0:T(8,128)(2,1)} %broadcast_in_dim.159), calls=%async_computation.3 | async-start | bytes 262144 | tf_op jit(solution)/shard_map/all_to_all | solution.py:50
  147.8 2.1 %fusion.34 = f32[512,128]{1,0:T(8,128)} fusion(bf16[512,1152]{1,0:T(8,128)(2,1)S(1)} %constant_dynamic-update-slice_fusion, bf16[3456,128]{1,0:T(8,128)(2,1)} %param.70), kind=kOutput, calls=%fused_computation.83 | convolution fusion | flops 150994944 | bytes 1736704 | tf_op jit(solution)/shard_map/dot_general | solution.py:130
  149.9 5.8 %all-to-all-done.3 = s16[8,64,128]{2,1,0:T(8,128)(2,1)} async-done(((s16[8,64,128]{2,1,0:T(8,128)(2,1)}), s16[8,64,128]{2,1,0:T(8,128)(2,1)}, u32[]{:S(2)}, u32[]{:S(2)}) %all-to-all-start.3) | async-done | bytes 131104 | tf_op jit(solution)/shard_map/all_to_all | solution.py:50
  158.7 6.5 %all-to-all-start.4 = ((s16[8,448,128]{2,1,0:T(8,128)(2,1)}), s16[8,448,128]{2,1,0:T(8,128)(2,1)S(1)}, u32[]{:S(2)}, u32[]{:S(2)}) async-start(s16[8,448,128]{2,1,0:T(8,128)(2,1)} %broadcast_in_dim.161), calls=%async_computation.4 | async-start | bytes 1835008 | tf_op jit(solution)/shard_map/all_to_all | solution.py:50
  166.8 2.1 %fusion.29 = bf16[1,512,128]{2,1,0:T(8,128)(2,1)} fusion(f32[512,128]{1,0:T(8,128)S(1)} %convolution_add_fusion.1, bf16[512,1152]{1,0:T(8,128)(2,1)S(1)} %copy-done.3, bf16[3456,128]{1,0:T(8,128)(2,1)} %param.70, bf16[1,512,128]{2,1,0:T(8,128)(2,1)S(1)} %copy-done.5, f32[512]{0:T(512)S(1)} %convert_element_type.181, bf16[512]{0:T(512)(128)(2,1)S(1)} %convert_reduce_fusion), kind=kOutput, calls=%fused_computation.75 | convolution fusion | flops 151388160 | bytes 2001920 | tf_op jit(solution)/shard_map/dot_general | solution.py:130
  171.8 7.0 %all-to-all-done.4 = s16[8,448,128]{2,1,0:T(8,128)(2,1)S(1)} async-done(((s16[8,448,128]{2,1,0:T(8,128)(2,1)}), s16[8,448,128]{2,1,0:T(8,128)(2,1)S(1)}, u32[]{:S(2)}, u32[]{:S(2)}) %all-to-all-start.4) | async-done | bytes 917536 | tf_op jit(solution)/shard_map/all_to_all | solution.py:50
  (227 shorter events, 53.7 us)
Async XLA Ops:
  3.6 6.5 %copy-start.1 = (bf16[3456,128]{1,0:T(8,128)(2,1)S(1)}, bf16[3456,128]{1,0:T(8,128)(2,1)}, u32[]{:S(2)}) copy-start(bf16[3456,128]{1,0:T(8,128)(2,1)} %param.70) | copy-start | bytes 2654212
  31.6 30.5 %collective-permute-start = (bf16[4,8192]{1,0:T(4,128)(2,1)S(1)}, bf16[4,8192]{1,0:T(4,128)(2,1)S(1)}, u32[]{:S(2)}, u32[]{:S(2)}) collective-permute-start(bf16[4,8192]{1,0:T(4,128)(2,1)S(1)} %pad_maximum_fusion), channel_id=1, source_target_pairs={{0,4},{4,0},{1,5},{5,1},{2,6},{6,2},{3,7},{7,3},{8,12},{12,8},{9,1... | collective-permute-start | bytes 196616 | tf_op jit(solution)/shard_map/ppermute | solution.py:28
  41.2 25.2 %collective-permute-start.1 = (bf16[4,8192]{1,0:T(4,128)(2,1)S(1)}, bf16[4,8192]{1,0:T(4,128)(2,1)S(1)}, u32[]{:S(2)}, u32[]{:S(2)}) collective-permute-start(bf16[4,8192]{1,0:T(4,128)(2,1)S(1)} %pad_maximum_fusion.1), channel_id=1, source_target_pairs={{0,8},{8,0},{16,24},{24,16},{32,40},{40,32},{48,56},{56,48},{1,9},... | collective-permute-start | bytes 196616 | tf_op jit(solution)/shard_map/ppermute | solution.py:28
  43.9 27.5 %collective-permute-start.2 = (bf16[4,8192]{1,0:T(4,128)(2,1)S(1)}, bf16[4,8192]{1,0:T(4,128)(2,1)S(1)}, u32[]{:S(2)}, u32[]{:S(2)}) collective-permute-start(bf16[4,8192]{1,0:T(4,128)(2,1)S(1)} %pad_maximum_fusion.2), channel_id=1, source_target_pairs={{0,16},{8,24},{16,0},{24,8},{32,48},{40,56},{48,32},{56,40},{1,17}... | collective-permute-start | bytes 196616 | tf_op jit(solution)/shard_map/ppermute | solution.py:28
  46.5 15.5 %copy-start.12 = (s32[6,6,6]{2,1,0:T(8,128)S(1)}, s32[6,6,6]{2,1,0:T(8,128)}, u32[]{:S(2)}) copy-start(s32[6,6,6]{2,1,0:T(8,128)} %constant.1055) | copy-start | bytes 2596
  47.3 24.8 %collective-permute-start.3 = (bf16[4,8192]{1,0:T(4,128)(2,1)S(1)}, bf16[4,8192]{1,0:T(4,128)(2,1)S(1)}, u32[]{:S(2)}, u32[]{:S(2)}) collective-permute-start(bf16[4,8192]{1,0:T(4,128)(2,1)S(1)} %pad_maximum_fusion.3), channel_id=1, source_target_pairs={{0,32},{8,40},{16,48},{24,56},{32,0},{40,8},{48,16},{56,24},{1,33}... | collective-permute-start | bytes 196616 | tf_op jit(solution)/shard_map/ppermute | solution.py:28
  56.1 17.3 %collective-permute-start.4 = (bf16[4,8192]{1,0:T(4,128)(2,1)S(1)}, bf16[4,8192]{1,0:T(4,128)(2,1)S(1)}, u32[]{:S(2)}, u32[]{:S(2)}) collective-permute-start(bf16[4,8192]{1,0:T(4,128)(2,1)S(1)} %pad_maximum_fusion.4), channel_id=1, source_target_pairs={{0,64},{64,0},{128,192},{192,128},{256,320},{320,256},{384,448},{4... | collective-permute-start | bytes 196616 | tf_op jit(solution)/shard_map/ppermute | solution.py:28
  62.1 10.6 %collective-permute-start.5 = (bf16[4,8192]{1,0:T(4,128)(2,1)S(1)}, bf16[4,8192]{1,0:T(4,128)(2,1)S(1)}, u32[]{:S(2)}, u32[]{:S(2)}) collective-permute-start(bf16[4,8192]{1,0:T(4,128)(2,1)S(1)} %pad_maximum_fusion.5), channel_id=1, source_target_pairs={{0,128},{64,192},{128,0},{192,64},{256,384},{320,448},{384,256},{4... | collective-permute-start | bytes 196616 | tf_op jit(solution)/shard_map/ppermute | solution.py:28
  66.4 9.0 %collective-permute-start.6 = (bf16[4,8192]{1,0:T(4,128)(2,1)S(1)}, bf16[4,8192]{1,0:T(4,128)(2,1)S(1)}, u32[]{:S(2)}, u32[]{:S(2)}) collective-permute-start(bf16[4,8192]{1,0:T(4,128)(2,1)S(1)} %pad_maximum_fusion.6), channel_id=1, source_target_pairs={{0,256},{64,320},{128,384},{192,448},{256,0},{320,64},{384,128},{4... | collective-permute-start | bytes 196616 | tf_op jit(solution)/shard_map/ppermute | solution.py:28
  73.4 7.3 %copy-start.11 = (bf16[4,8192]{1,0:T(4,128)(2,1)}, bf16[4,8192]{1,0:T(4,128)(2,1)S(1)}, u32[]{:S(2)}) copy-start(bf16[4,8192]{1,0:T(4,128)(2,1)S(1)} %collective-permute-done.4) | copy-start | bytes 196612
  83.4 0.9 copy-start
  84.4 1.0 copy-start.2
  89.0 20.7 %all-to-all-start = ((s16[8,448,128]{2,1,0:T(8,128)(2,1)}), s16[8,448,128]{2,1,0:T(8,128)(2,1)}, u32[]{:S(2)}, u32[]{:S(2)}) async-start(s16[8,448,128]{2,1,0:T(8,128)(2,1)} %add_add_fusion), calls=%async_computation | async-start | bytes 1835008 | tf_op jit(solution)/shard_map/all_to_all | solution.py:50
  112.7 17.2 %copy-start.10 = (s32[1,1,256]{2,1,0:T(1,128)S(1)}, s32[1,1,256]{2,1,0:T(1,128)}, u32[]{:S(2)}) copy-start(s32[1,1,256]{2,1,0:T(1,128)} %param.68) | copy-start | bytes 3076
  113.8 16.5 %copy-start.6 = (bf16[2,8192]{1,0:T(2,128)(2,1)S(1)}, bf16[2,8192]{1,0:T(2,128)(2,1)}, u32[]{:S(2)}) copy-start(bf16[2,8192]{1,0:T(2,128)(2,1)} %get-tuple-element.386) | copy-start | bytes 98308
  113.8 16.5 %copy-start.7 = (bf16[2,8192]{1,0:T(2,128)(2,1)S(1)}, bf16[2,8192]{1,0:T(2,128)(2,1)}, u32[]{:S(2)}) copy-start(bf16[2,8192]{1,0:T(2,128)(2,1)} %get-tuple-element.388) | copy-start | bytes 98308
  125.6 15.6 %all-to-all-start.2 = ((s16[8,64,128]{2,1,0:T(8,128)(2,1)}), s16[8,64,128]{2,1,0:T(8,128)(2,1)}, u32[]{:S(2)}, u32[]{:S(2)}) async-start(s16[8,64,128]{2,1,0:T(8,128)(2,1)} %broadcast_in_dim.158), calls=%async_computation.2 | async-start | bytes 262144 | tf_op jit(solution)/shard_map/all_to_all | solution.py:50
  132.1 3.9 %copy-start.8 = (bf16[2,8192]{1,0:T(2,128)(2,1)S(1)}, bf16[2,8192]{1,0:T(2,128)(2,1)}, u32[]{:S(2)}) copy-start(bf16[2,8192]{1,0:T(2,128)(2,1)} %get-tuple-element.378) | copy-start | bytes 98308
  132.1 3.9 %copy-start.9 = (bf16[2,8192]{1,0:T(2,128)(2,1)S(1)}, bf16[2,8192]{1,0:T(2,128)(2,1)}, u32[]{:S(2)}) copy-start(bf16[2,8192]{1,0:T(2,128)(2,1)} %get-tuple-element.380) | copy-start | bytes 98308
  143.8 11.9 %all-to-all-start.3 = ((s16[8,64,128]{2,1,0:T(8,128)(2,1)}), s16[8,64,128]{2,1,0:T(8,128)(2,1)}, u32[]{:S(2)}, u32[]{:S(2)}) async-start(s16[8,64,128]{2,1,0:T(8,128)(2,1)} %broadcast_in_dim.159), calls=%async_computation.3 | async-start | bytes 262144 | tf_op jit(solution)/shard_map/all_to_all | solution.py:50
  157.6 7.5 %copy-start.4 = (f32[512,128]{1,0:T(8,128)S(1)}, f32[512,128]{1,0:T(8,128)}, u32[]{:S(2)}) copy-start(f32[512,128]{1,0:T(8,128)} %fusion.34) | copy-start | bytes 786436
  158.7 20.0 %all-to-all-start.4 = ((s16[8,448,128]{2,1,0:T(8,128)(2,1)}), s16[8,448,128]{2,1,0:T(8,128)(2,1)S(1)}, u32[]{:S(2)}, u32[]{:S(2)}) async-start(s16[8,448,128]{2,1,0:T(8,128)(2,1)} %broadcast_in_dim.161), calls=%async_computation.4 | async-start | bytes 1835008 | tf_op jit(solution)/shard_map/all_to_all | solution.py:50
  165.2 1.6 copy-start.3
  165.2 1.6 copy-start.5

commit v2 on v1

v2 whole, which is shorter than its diff:
```python
import functools
import math

import jax
import jax.numpy as jnp
from jax import lax
from jax.experimental import pallas as pl
from jax.experimental.pallas import tpu as pltpu
from jax.sharding import Mesh, PartitionSpec as P


SPACE = ("y", "z", "core")
FULL = 16383.0
FULL_BITS = 14
SHARD_ROWS = 64
SPARE = 16


def bit_axes(sizes):
    steps = []
    for axis in reversed(SPACE):
        for bit in range(sizes[axis].bit_length() - 1):
            steps.append((axis, bit))
    return steps


def swapped(value, step):
    axis, bit = step
    pairs = [(source, source ^ 2**bit) for source in range(lax.axis_size(axis))]
    return lax.ppermute(value, axis, pairs)


def encode(values, extra=None):
    rows = values.shape[-2]
    peak = jnp.max(jnp.abs(values), axis=-2, keepdims=True)
    power = jnp.clip(jnp.ceil(jnp.log2(jnp.maximum(peak, 1e-30))), -100.0, 100.0)
    coded = jnp.round(values * jnp.exp2(FULL_BITS - power)).astype(jnp.int16)
    spare = [power.astype(jnp.int16)]
    if extra is not None:
        spare.append(jnp.broadcast_to(extra.astype(jnp.int16), power.shape))
    fill = -rows % SPARE or SPARE
    spare.append(jnp.zeros(values.shape[:-2] + (fill - len(spare), values.shape[-1]), jnp.int16))
    return jnp.concatenate([coded] + spare, axis=-2)


def decode(coded, rows):
    power = coded[..., rows : rows + 1, :].astype(jnp.float32)
    return coded[..., :rows, :].astype(jnp.float32) * jnp.exp2(power - FULL_BITS)


def exchanged(parts, axes):
    return lax.all_to_all(parts, axes, 0, 0, tiled=True)


def everyone(part, axes, count):
    return exchanged(jnp.broadcast_to(part[None], (count,) + part.shape), axes)


def reduced(weighted, own_weight):
    rows, channels = weighted.shape
    near = ("core", "x")
    near_count = lax.axis_size("core") * lax.axis_size("x")
    depth = lax.axis_size("z")
    breadth = lax.axis_size("y")
    near_rows = rows // near_count
    own_rows = near_rows // depth
    parts = exchanged(encode(weighted.reshape(near_count, near_rows, channels), own_weight), near)
    total_weight = jnp.sum(parts[:, near_rows + 1, 0].astype(jnp.float32)) / lax.axis_size("core")
    part = jnp.sum(decode(parts, near_rows), axis=0)
    parts = exchanged(encode(part.reshape(depth, own_rows, channels)), "z")
    part = jnp.sum(decode(parts, own_rows), axis=0)
    parts = everyone(encode(part), "y", breadth)
    part = jnp.sum(decode(parts, own_rows), axis=0)
    part = decode(everyone(encode(part), "z", depth), own_rows).reshape(near_rows, channels)
    whole = decode(everyone(encode(part), near, near_count), near_rows).reshape(rows, channels)
    return whole, total_weight


def halo_place(pair_table, device, bricks, nspace, peer_cap, levels):
    relative = jnp.clip(pair_table - bricks, 0, nspace * peer_cap - 1)
    flipped = jnp.bitwise_xor(relative // peer_cap, device)
    level_of = jnp.zeros_like(pair_table)
    for bit_level in range(levels):
        level_of = level_of + bit_level * (flipped == 1 << bit_level).astype(jnp.int32)
    kind = jnp.where(
        pair_table < bricks, 0, jnp.where(pair_table >= bricks + nspace * peer_cap, 2, 1)
    )
    return kind, level_of, relative % peer_cap


def voxel_sources():
    sources = []
    for pos in range(6):
        step = (pos - 1) // 4
        sources.append((step + 1, pos - 1 - 4 * step))
    return sources


SOURCES = voxel_sources()


def onehot(left, right, dtype=jnp.bfloat16):
    return jnp.where(left == right, 1.0, 0.0).astype(dtype)


def stacked_rows(rows):
    channels = rows.shape[1] // 64
    return jnp.concatenate(
        [
            rows[:, (xy * 4 + z) * channels : (xy * 4 + z + 1) * channels]
            for z in range(4)
            for xy in range(16)
        ],
        axis=0,
    )


def backward_kernel(levels, grad_ref, own_ref, kernel_ref, rows_ref, pick_ref, *refs):
    send_refs = refs[:levels]
    own_grad_ref, cube_ref, table_ref = refs[levels:]
    bricks = grad_ref.shape[0]
    channels = kernel_ref.shape[1]
    wide = 4 * channels
    grad = grad_ref[...].astype(jnp.float32)
    stacked = stacked_rows(grad).astype(jnp.bfloat16)
    cube_ref[...] = jnp.zeros_like(cube_ref)
    for tap in range(9):
        tap_x, tap_y = tap // 3, tap % 3
        weight = kernel_ref[tap * 3 * channels : (tap + 1) * 3 * channels, :]
        part = lax.dot_general(
            stacked, weight, (((1,), (1,)), ((), ())), preferred_element_type=jnp.float32
        )
        for z in range(4):
            for x in range(4):
                for y in range(4):
                    row = (z * 16 + x * 4 + y) * bricks
                    cube_ref[
                        (x + tap_x) * 6 + y + tap_y, :, z * channels : (z + 3) * channels
                    ] += part[row : row + bricks]
    table_rows = table_ref.shape[0]
    slots = lax.broadcasted_iota(jnp.int32, (table_rows, 2 * bricks), 0)
    chooser = [
        onehot(slots, jnp.broadcast_to(rows_ref[offset : offset + 1, :], slots.shape))
        for offset in range(27)
    ]
    for xy in range(16):
        total = None
        low = None
        high = None
        for pos_x in range(6):
            for pos_y in range(6):
                if (SOURCES[pos_x][1], SOURCES[pos_y][1]) != (xy // 4, xy % 4):
                    continue
                base = 9 * SOURCES[pos_x][0] + 3 * SOURCES[pos_y][0]
                piece = cube_ref[pos_x * 6 + pos_y]
                upper = piece.astype(jnp.bfloat16)
                lower = (piece - upper.astype(jnp.float32)).astype(jnp.bfloat16)
                both = jnp.concatenate([upper, lower], axis=0)

                def spread(offset, start, stop):
                    return jnp.dot(
                        chooser[offset], both[:, start:stop], preferred_element_type=jnp.float32
                    )

                mid = spread(base + 1, channels, 5 * channels)
                first = spread(base + 2, 5 * channels, 6 * channels)
                last = spread(base, 0, channels)
                total = mid if total is None else total + mid
                low = first if low is None else low + first
                high = last if high is None else high + last
        start = xy * wide
        table_ref[:, start : start + channels] = total[:, :channels] + low
        table_ref[:, start + channels : start + 3 * channels] = total[:, channels : 3 * channels]
        table_ref[:, start + 3 * channels : start + wide] = total[:, 3 * channels :] + high
    pick_rows = pick_ref.shape[0]
    lanes = lax.broadcasted_iota(jnp.int32, (pick_rows, bricks), 1)
    picker = onehot(lanes, jnp.broadcast_to(pick_ref[...], lanes.shape))
    for xy in range(16):
        span = slice(xy * wide, (xy + 1) * wide)
        sent = table_ref[:pick_rows, span] + jnp.dot(
            picker, own_ref[:, span], preferred_element_type=jnp.float32
        )
        for level in range(levels):
            send_refs[level][:, span] = sent[4 * level : 4 * level + 4].astype(jnp.bfloat16)
        own_grad_ref[:, span] = table_ref[pick_rows:, span] + grad[:, span]


def patch_kernel(table_ref, grad_ref, rows_ref, weight_ref, cube_ref):
    bricks = grad_ref.shape[0]
    table_rows = table_ref.shape[0]
    channels = weight_ref.shape[1]
    wide = 4 * channels
    lanes = lax.broadcasted_iota(jnp.int32, (27 * bricks, table_rows), 1)
    chooser = onehot(lanes, jnp.broadcast_to(rows_ref[...], lanes.shape), jnp.float32)
    for xy in range(16):
        places = [
            (pos_x, pos_y)
            for pos_x in range(6)
            for pos_y in range(6)
            if (SOURCES[pos_x][1], SOURCES[pos_y][1]) == (xy // 4, xy % 4)
        ]

        def picked(side, start, stop):
            rows = []
            for pos_x, pos_y in places:
                offset = 9 * SOURCES[pos_x][0] + 3 * SOURCES[pos_y][0] + side
                rows.append(chooser[offset * bricks : (offset + 1) * bricks])
            rows = rows[0] if len(rows) == 1 else jnp.concatenate(rows, axis=0)
            return jnp.dot(
                rows.astype(jnp.bfloat16),
                table_ref[:, xy * wide + start : xy * wide + stop],
                preferred_element_type=jnp.float32,
            )

        first = picked(0, 3 * channels, wide)
        mid = picked(1, 0, wide)
        last = picked(2, 0, channels)
        for at, (pos_x, pos_y) in enumerate(places):
            rows = slice(at * bricks, (at + 1) * bricks)
            cube_ref[pos_x * 6 + pos_y, :, :channels] = first[rows]
            cube_ref[pos_x * 6 + pos_y, :, channels : 5 * channels] = mid[rows]
            cube_ref[pos_x * 6 + pos_y, :, 5 * channels :] = last[rows]
    turned = stacked_rows(grad_ref[...].astype(jnp.float32)).T.astype(jnp.bfloat16)
    for tap in range(9):
        part = jnp.dot(turned, columns_of(cube_ref, tap), preferred_element_type=jnp.float32)
        for tap_z in range(3):
            row = (tap * 3 + tap_z) * channels
            weight_ref[row : row + channels, :] = part[:, tap_z * channels : (tap_z + 1) * channels].T


def columns_of(cube_ref, tap):
    channels = cube_ref.shape[2] // 6
    tap_x, tap_y = tap // 3, tap % 3
    slab = jnp.concatenate(
        [cube_ref[(x + tap_x) * 6 + y + tap_y] for x in range(4) for y in range(4)], axis=0
    ).astype(jnp.bfloat16)
    return jnp.concatenate(
        [slab[:, z * channels : (z + 3) * channels] for z in range(4)], axis=0
    )


def forward_kernel(
    cube_ref, kernel_ref, table_ref, own_ref, own_grad_ref, back_ref, mask_ref, out_ref, sum_ref
):
    bricks = own_ref.shape[0]
    channels = kernel_ref.shape[1]
    total = None
    for tap in range(9):
        part = jnp.dot(
            columns_of(cube_ref, tap),
            kernel_ref[tap * 3 * channels : (tap + 1) * 3 * channels, :],
            preferred_element_type=jnp.float32,
        )
        total = part if total is None else total + part
    owners = lax.broadcasted_iota(jnp.int32, (bricks, table_ref.shape[0]), 0)
    backer = onehot(owners, jnp.broadcast_to(back_ref[...], owners.shape))
    for xy in range(16):
        for z in range(4):
            voxel = xy * 4 + z
            span = slice(voxel * channels, (voxel + 1) * channels)
            row = (z * 16 + xy) * bricks
            mask = jnp.broadcast_to(mask_ref[:, voxel : voxel + 1], (bricks, channels))
            own = own_ref[:, span].astype(jnp.float32)
            out_ref[:, span] = (mask * (total[row : row + bricks] + own)).astype(jnp.bfloat16)
            back = jnp.dot(backer, table_ref[:, span], preferred_element_type=jnp.float32)
            sum_ref[:, span] = mask * (own_grad_ref[:, span] + back)


def local_call(body, out_shape, scratch, flops, moved):
    return pl.pallas_call(
        body,
        out_shape=out_shape,
        scratch_shapes=scratch,
        compiler_params=pltpu.CompilerParams(vmem_limit_bytes=40 * 1024 * 1024),
        cost_estimate=pl.CostEstimate(flops=flops, bytes_accessed=moved, transcendentals=0),
    )


def on_device(features, occupancy, brick_pairs, send_lists, scan_weight, kernel, cotangent):
    channels = features.shape[2]
    own_rows = features.shape[1]
    bricks = own_rows // 64
    nspace = lax.axis_size(SPACE)
    scan_count = lax.axis_size("x")
    steps = bit_axes({axis: lax.axis_size(axis) for axis in SPACE})
    levels = len(steps)
    device = lax.axis_index(SPACE)
    send_table = send_lists[0, 0]
    peer_cap = send_table.shape[0] // nspace
    assert peer_cap == 2 and bricks == 8
    send_rows = -(-4 * levels // 8) * 8
    table_rows = send_rows + bricks
    width = 64 * channels
    voxel_mask = occupancy[0][:, None].astype(jnp.bfloat16)
    masked = (features[0] * voxel_mask).reshape(bricks, width)
    grad_in = (cotangent[0] * voxel_mask).reshape(bricks, width)
    mask_float = occupancy[0].reshape(bricks, 64).astype(jnp.float32)
    kind, level_of, within = halo_place(brick_pairs[0].T, device, bricks, nspace, peer_cap, levels)
    pair_table = brick_pairs[0].T
    forward_rows = jnp.where(
        kind == 0, send_rows + pair_table, jnp.where(kind == 1, 4 * level_of + within, -1)
    )
    backward_rows = jnp.where(kind == 1, forward_rows + peer_cap, forward_rows)
    backward_rows = jnp.concatenate([backward_rows, backward_rows], axis=1)
    forward_rows = forward_rows.reshape(27 * bricks, 1)
    partners = jnp.bitwise_xor(device, jnp.left_shift(1, jnp.arange(levels, dtype=jnp.int32)))
    entries = partners[:, None] * peer_cap + jnp.arange(peer_cap, dtype=jnp.int32)[None, :]
    chosen = jnp.take(send_table, entries.reshape(-1)).reshape(levels, peer_cap)
    nothing = jnp.full((levels, peer_cap), -1, jnp.int32)
    pick_rows = jnp.pad(
        jnp.concatenate([chosen, nothing], axis=1).reshape(-1),
        (0, send_rows - 4 * levels),
        constant_values=-1,
    ).reshape(send_rows, 1)
    back_rows = jnp.pad(
        jnp.concatenate([nothing, chosen], axis=1).reshape(-1),
        (0, table_rows - 4 * levels),
        constant_values=-1,
    ).reshape(1, table_rows)
    macs = own_rows * 27 * channels * channels
    cube = (36, bricks, 6 * channels)
    *sends, own_grad = local_call(
        functools.partial(backward_kernel, levels),
        [jax.ShapeDtypeStruct((4, width), jnp.bfloat16)] * levels
        + [jax.ShapeDtypeStruct((bricks, width), jnp.float32)],
        [pltpu.VMEM(cube, jnp.float32), pltpu.VMEM((table_rows, width), jnp.float32)],
        2 * macs,
        4 * 2**20,
    )(grad_in, masked, kernel, backward_rows, pick_rows)
    came = [swapped(sends[level], steps[level]) for level in range(levels)]
    blank = jnp.zeros((send_rows - 4 * levels, width), jnp.bfloat16)
    table = jnp.concatenate(came + [blank, masked], axis=0)
    weight_grad, cubes = local_call(
        patch_kernel,
        [
            jax.ShapeDtypeStruct(kernel.shape, jnp.float32),
            jax.ShapeDtypeStruct(cube, jnp.float32),
        ],
        [],
        2 * macs,
        4 * 2**20,
    )(table, grad_in, forward_rows)
    output, grad_sum = local_call(
        forward_kernel,
        [
            jax.ShapeDtypeStruct((bricks, width), jnp.bfloat16),
            jax.ShapeDtypeStruct((bricks, width), jnp.float32),
        ],
        [],
        2 * macs,
        4 * 2**20,
    )(cubes, kernel, table, masked, own_grad, back_rows, mask_float)
    own_weight = scan_weight[0].astype(jnp.float32)
    summed, weight_total = reduced(weight_grad * own_weight, own_weight)
    factor = own_weight * scan_count / weight_total
    grad_features = (factor * grad_sum).astype(jnp.bfloat16)
    kernel_grad = summed * (scan_count / weight_total) / math.sqrt(64.0 * bricks * nspace)
    return (
        output.reshape(1, own_rows, channels),
        grad_features.reshape(1, own_rows, channels),
        kernel_grad,
    )


def solution(mesh):
    sizes = dict(mesh.shape)
    assert mesh.axis_names == ("space", "dp")
    inner = Mesh(
        mesh.devices.reshape(8, sizes["space"] // 16, 2, sizes["dp"]), ("y", "z", "core", "x")
    )
    return jax.shard_map(
        on_device,
        mesh=inner,
        in_specs=(
            P("x", SPACE, None),
            P("x", SPACE),
            P("x", SPACE, None),
            P("x", SPACE, None),
            P("x"),
            P(),
            P("x", SPACE, None),
        ),
        out_specs=(P("x", SPACE, None), P("x", SPACE, None), P()),
        check_vma=False,
    )
```

time: 182 us -> 134 us (0.74)
  other arithmetic: 38 us -> 8.29 us
  local copies, waits for them, and re-layouts: 28.5 us -> 9.65 us
  matrix products: 16.1 us -> 0 us
  waiting for transfers between devices: 28.3 us -> 41.2 us
  Pallas kernels: 0 us -> 4.87 us
    dot_general x33 -> x0, matrix products: 16.1 us -> none  [the longest x27 8.51 us: gradients(): jnp.dot(grad_in, tap_weight.T, preferred_element_type=jnp.float32)]
    scatter-add x2 -> x0, other arithmetic: 13.6 us -> none  [the longest x1 11.8 us: gradients(): jax.ops.segment_sum(patch_grad.reshape(-1, channels), patch_rows.reshape(...]
    all_to_all x4, waiting for transfers between devices: 26.3 us -> 37.9 us  [exchanged(): return lax.all_to_all(parts, axes, 0, 0, tiled=True)]
    gather x11 -> x2, local copies, waits for them, and re-layouts: 8.97 us -> 0.74 us  [on_device(): chosen = jnp.take(send_table, entries.reshape(-1)).reshape(levels, peer_cap)]
    add x4 -> x1, other arithmetic: 7.19 us -> 0.07 us  [on_device(): partners[:, None] * peer_cap]
    slice x11 -> x0, local copies, waits for them, and re-layouts: 6.44 us -> none  [the longest x6 2.74 us: on_device(): came[peer_cap:].astype(jnp.float32)]
    pallas_call x0 -> x3, Pallas kernels: none -> 4.87 us  [the longest x1 2.28 us: on_device(): local_call(functools.partial(backward_kernel, levels), [jax.ShapeDtypeStr...]
  transfers between devices with their start and end apart: 11 -> 11, of which waited for: 4 -> 5; matrix products, arithmetic and copies ran while one was open for 15% -> 3% of each run, Pallas kernels for 0% -> 1%
where the time goes in v2:
time: 134 us; the launch traced here: 133 us
  starting transfers between devices  55.6 us (41%)
  waiting for transfers between devices  41.2 us (31%)
  blocking collectives  10.8 us (8%)
  local copies, waits for them, and re-layouts  9.65 us (7%)
  other arithmetic  8.29 us (6%)
  Pallas kernels  4.87 us (4%)
  between operations  2.4 us (2%)
    all_to_all x4, waiting for transfers between devices, exchanged(): return lax.all_to_all(parts, axes, 0, 0, tiled=True)  37.9 us
    ppermute x7, starting transfers between devices, swapped(): return lax.ppermute(value, axis, pairs)  33.3 us
    all_to_all x4, starting transfers between devices, exchanged(): return lax.all_to_all(parts, axes, 0, 0, tiled=True)  22.2 us
    all_to_all x1, blocking collectives, exchanged(): return lax.all_to_all(parts, axes, 0, 0, tiled=True)  10.8 us
    ppermute x7, waiting for transfers between devices, swapped(): return lax.ppermute(value, axis, pairs)  3.34 us
  transfers between devices with their start and end apart: 11, of which 5 were waited for; matrix products, arithmetic and copies ran while one was open for 3% of the time, Pallas kernels for 1%

profile of v2, /device:TPU:1, one launch (start us, length us, event | category | flops | bytes accessed | tf_op | source)
XLA Modules:
  0.0 132.9 jit_solution(14474520424428499051)
XLA Ops:
  5.9 2.3 %shard_map.94 = (bf16[4,8192]{1,0:T(4,128)(2,1)S(1)}, bf16[4,8192]{1,0:T(4,128)(2,1)S(1)}, bf16[4,8192]{1,0:T(4,128)(2,1)S(1)}, bf16[4,8192]{1,0:T(4,128)(2,1)S(...) custom-call(bf16[8,8192]{1,0:T(8,128)(2,1)S(1)} %get-tuple-element.3, ...), custom_call_target="tpu_custom_call" | custom-call | flops 452984832 | bytes 4194304 | tf_op jit(solution)/shard_map/pallas_call | solution.py:322
  8.2 8.7 %collective-permute-start = (bf16[4,8192]{1,0:T(4,128)(2,1)S(1)}, bf16[4,8192]{1,0:T(4,128)(2,1)S(1)}, u32[]{:S(2)}, u32[]{:S(2)}) collective-permute-start(bf16[4,8192]{1,0:T(4,128)(2,1)S(1)} %get-tuple-element.15), channel_id=1, source_target_pairs={{0,4},{4,0},{1,5},{5,1},{2,6},{6,2},{3,7},{7,3},{8,12},{12,8},{9,1... | collective-permute-start | bytes 196616 | tf_op jit(solution)/shard_map/ppermute | solution.py:30
  16.9 1.9 %collective-permute-start.1 = (bf16[4,8192]{1,0:T(4,128)(2,1)S(1)}, bf16[4,8192]{1,0:T(4,128)(2,1)S(1)}, u32[]{:S(2)}, u32[]{:S(2)}) collective-permute-start(bf16[4,8192]{1,0:T(4,128)(2,1)S(1)} %get-tuple-element.16), channel_id=1, source_target_pairs={{0,8},{8,0},{16,24},{24,16},{32,40},{40,32},{48,56},{56,48},{1,9},... | collective-permute-start | bytes 196616 | tf_op jit(solution)/shard_map/ppermute | solution.py:30
  18.8 2.5 %collective-permute-start.2 = (bf16[4,8192]{1,0:T(4,128)(2,1)S(1)}, bf16[4,8192]{1,0:T(4,128)(2,1)S(1)}, u32[]{:S(2)}, u32[]{:S(2)}) collective-permute-start(bf16[4,8192]{1,0:T(4,128)(2,1)S(1)} %get-tuple-element.17), channel_id=1, source_target_pairs={{0,16},{8,24},{16,0},{24,8},{32,48},{40,56},{48,32},{56,40},{1,17}... | collective-permute-start | bytes 196616 | tf_op jit(solution)/shard_map/ppermute | solution.py:30
  21.4 7.9 %collective-permute-start.3 = (bf16[4,8192]{1,0:T(4,128)(2,1)S(1)}, bf16[4,8192]{1,0:T(4,128)(2,1)S(1)}, u32[]{:S(2)}, u32[]{:S(2)}) collective-permute-start(bf16[4,8192]{1,0:T(4,128)(2,1)S(1)} %get-tuple-element.18), channel_id=1, source_target_pairs={{0,32},{8,40},{16,48},{24,56},{32,0},{40,8},{48,16},{56,24},{1,33}... | collective-permute-start | bytes 196616 | tf_op jit(solution)/shard_map/ppermute | solution.py:30
  29.3 3.2 %collective-permute-start.4 = (bf16[4,8192]{1,0:T(4,128)(2,1)S(1)}, bf16[4,8192]{1,0:T(4,128)(2,1)S(1)}, u32[]{:S(2)}, u32[]{:S(2)}) collective-permute-start(bf16[4,8192]{1,0:T(4,128)(2,1)S(1)} %get-tuple-element.19), channel_id=1, source_target_pairs={{0,64},{64,0},{128,192},{192,128},{256,320},{320,256},{384,448},{4... | collective-permute-start | bytes 196616 | tf_op jit(solution)/shard_map/ppermute | solution.py:30
  32.6 4.2 %collective-permute-start.5 = (bf16[4,8192]{1,0:T(4,128)(2,1)S(1)}, bf16[4,8192]{1,0:T(4,128)(2,1)S(1)}, u32[]{:S(2)}, u32[]{:S(2)}) collective-permute-start(bf16[4,8192]{1,0:T(4,128)(2,1)S(1)} %get-tuple-element.20), channel_id=1, source_target_pairs={{0,128},{64,192},{128,0},{192,64},{256,384},{320,448},{384,256},{4... | collective-permute-start | bytes 196616 | tf_op jit(solution)/shard_map/ppermute | solution.py:30
  36.8 4.7 %collective-permute-start.6 = (bf16[4,8192]{1,0:T(4,128)(2,1)S(1)}, bf16[4,8192]{1,0:T(4,128)(2,1)S(1)}, u32[]{:S(2)}, u32[]{:S(2)}) collective-permute-start(bf16[4,8192]{1,0:T(4,128)(2,1)S(1)} %get-tuple-element.21), channel_id=1, source_target_pairs={{0,256},{64,320},{128,384},{192,448},{256,0},{320,64},{384,128},{4... | collective-permute-start | bytes 196616 | tf_op jit(solution)/shard_map/ppermute | solution.py:30
  42.5 3.3 %collective-permute-done.6 = bf16[4,8192]{1,0:T(4,128)(2,1)S(1)} collective-permute-done((bf16[4,8192]{1,0:T(4,128)(2,1)S(1)}, bf16[4,8192]{1,0:T(4,128)(2,1)S(1)}, u32[]{:S(2)}, u32[]{:S(2)}) %collective-permute-start.6) | collective-permute-done | bytes 65568 | tf_op jit(solution)/shard_map/ppermute | solution.py:30
  46.2 1.3 shard_map.95
  48.1 1.3 add_add_fusion
  49.4 7.1 %all-to-all-start = ((s16[8,448,128]{2,1,0:T(8,128)(2,1)}), s16[8,448,128]{2,1,0:T(8,128)(2,1)}, u32[]{:S(2)}, u32[]{:S(2)}) async-start(s16[8,448,128]{2,1,0:T(8,128)(2,1)} %add_add_fusion), calls=%async_computation | async-start | bytes 1835008 | tf_op jit(solution)/shard_map/all_to_all | solution.py:52
  56.5 13.6 %all-to-all-done = s16[8,448,128]{2,1,0:T(8,128)(2,1)} async-done(((s16[8,448,128]{2,1,0:T(8,128)(2,1)}), s16[8,448,128]{2,1,0:T(8,128)(2,1)}, u32[]{:S(2)}, u32[]{:S(2)}) %all-to-all-start) | async-done | bytes 917536 | tf_op jit(solution)/shard_map/all_to_all | solution.py:52
  70.8 1.5 %multiply_reduce_fusion = f32[432,128]{1,0:T(8,128)S(1)} fusion(s16[8,448,128]{2,1,0:T(8,128)(2,1)} %all-to-all-done, f32[8,128]{1,0:T(8,128)S(1)} %exponential_bitcast_fusion.4), kind=kLoop, calls=%fused_computation.2 | loop fusion | flops 1271808 | bytes 1110016 | tf_op jit(solution)/shard_map/reduce_sum | solution.py:69
  72.6 10.8 %all_to_all.25 = s16[8,64,128]{2,1,0:T(8,128)(2,1)S(1)} all-to-all(s16[8,64,128]{2,1,0:T(8,128)(2,1)S(1)} %add_add_fusion.1), channel_id=1, replica_groups=mesh['y'=8,'z'=8,'core'=2,'x'=4] {'z'}, dimensions={0} | all-to-all | bytes 262144 | tf_op jit(solution)/shard_map/all_to_all | solution.py:52
  84.3 4.3 %all-to-all-start.2 = ((s16[8,64,128]{2,1,0:T(8,128)(2,1)}), s16[8,64,128]{2,1,0:T(8,128)(2,1)S(1)}, u32[]{:S(2)}, u32[]{:S(2)}) async-start(s16[8,64,128]{2,1,0:T(8,128)(2,1)} %broadcast_in_dim.78), calls=%async_computation.2 | async-start | bytes 262144 | tf_op jit(solution)/shard_map/all_to_all | solution.py:52
  88.9 7.7 %all-to-all-done.2 = s16[8,64,128]{2,1,0:T(8,128)(2,1)S(1)} async-done(((s16[8,64,128]{2,1,0:T(8,128)(2,1)}), s16[8,64,128]{2,1,0:T(8,128)(2,1)S(1)}, u32[]{:S(2)}, u32[]{:S(2)}) %all-to-all-start.2) | async-done | bytes 131104 | tf_op jit(solution)/shard_map/all_to_all | solution.py:52
  97.5 3.4 %all-to-all-start.3 = ((s16[8,64,128]{2,1,0:T(8,128)(2,1)}), s16[8,64,128]{2,1,0:T(8,128)(2,1)S(1)}, u32[]{:S(2)}, u32[]{:S(2)}) async-start(s16[8,64,128]{2,1,0:T(8,128)(2,1)} %broadcast_in_dim.79), calls=%async_computation.3 | async-start | bytes 262144 | tf_op jit(solution)/shard_map/all_to_all | solution.py:52
  100.8 1.3 shard_map.96
  102.9 1.3 %fusion.10 = f32[]{:T(128)} fusion(s16[8,448,128]{2,1,0:T(8,128)(2,1)} %all-to-all-done), kind=kLoop, calls=%fused_computation.48 | loop fusion | flops 15 | bytes 20 | tf_op jit(solution)/shard_map/reduce_sum | solution.py:68
  104.9 3.9 %all-to-all-done.3 = s16[8,64,128]{2,1,0:T(8,128)(2,1)S(1)} async-done(((s16[8,64,128]{2,1,0:T(8,128)(2,1)}), s16[8,64,128]{2,1,0:T(8,128)(2,1)S(1)}, u32[]{:S(2)}, u32[]{:S(2)}) %all-to-all-start.3) | async-done | bytes 131104 | tf_op jit(solution)/shard_map/all_to_all | solution.py:52
  110.1 7.5 %all-to-all-start.4 = ((s16[8,448,128]{2,1,0:T(8,128)(2,1)}), s16[8,448,128]{2,1,0:T(8,128)(2,1)S(1)}, u32[]{:S(2)}, u32[]{:S(2)}) async-start(s16[8,448,128]{2,1,0:T(8,128)(2,1)} %broadcast_in_dim.81), calls=%async_computation.4 | async-start | bytes 1835008 | tf_op jit(solution)/shard_map/all_to_all | solution.py:52
  118.4 12.8 %all-to-all-done.4 = s16[8,448,128]{2,1,0:T(8,128)(2,1)S(1)} async-done(((s16[8,448,128]{2,1,0:T(8,128)(2,1)}), s16[8,448,128]{2,1,0:T(8,128)(2,1)S(1)}, u32[]{:S(2)}, u32[]{:S(2)}) %all-to-all-start.4) | async-done | bytes 917536 | tf_op jit(solution)/shard_map/all_to_all | solution.py:52
  131.2 1.6 %multiply_multiply_fusion = f32[8,432,128]{2,1,0:T(8,128)} fusion(s16[8,448,128]{2,1,0:T(8,128)(2,1)S(1)} %all-to-all-done.4, f32[]{:T(128)S(6)} %div.32, f32[8,128]{1,0:T(8,128)S(1)} %exponential_bitcast_fusion), kind=kLoop, calls=%fused_computation.1 | loop fusion | flops 1769472 | bytes 2658308 | tf_op jit(solution)/shard_map/div | solution.py:357
  (89 shorter events, 12.2 us)
Async XLA Ops:
  0.6 4.0 %copy-start = (s32[1,1,256]{2,1,0:T(1,128)S(1)}, s32[1,1,256]{2,1,0:T(1,128)}, u32[]{:S(2)}) copy-start(s32[1,1,256]{2,1,0:T(1,128)} %param.10) | copy-start | bytes 3076
  0.6 5.2 %copy-start.1 = (bf16[3456,128]{1,0:T(8,128)(2,1)S(1)}, bf16[3456,128]{1,0:T(8,128)(2,1)}, u32[]{:S(2)}) copy-start(bf16[3456,128]{1,0:T(8,128)(2,1)} %kernel_ref.3) | copy-start | bytes 2654212
  8.2 24.4 %collective-permute-start = (bf16[4,8192]{1,0:T(4,128)(2,1)S(1)}, bf16[4,8192]{1,0:T(4,128)(2,1)S(1)}, u32[]{:S(2)}, u32[]{:S(2)}) collective-permute-start(bf16[4,8192]{1,0:T(4,128)(2,1)S(1)} %get-tuple-element.15), channel_id=1, source_target_pairs={{0,4},{4,0},{1,5},{5,1},{2,6},{6,2},{3,7},{7,3},{8,12},{12,8},{9,1... | collective-permute-start | bytes 196616 | tf_op jit(solution)/shard_map/ppermute | solution.py:30
  16.9 19.9 %collective-permute-start.1 = (bf16[4,8192]{1,0:T(4,128)(2,1)S(1)}, bf16[4,8192]{1,0:T(4,128)(2,1)S(1)}, u32[]{:S(2)}, u32[]{:S(2)}) collective-permute-start(bf16[4,8192]{1,0:T(4,128)(2,1)S(1)} %get-tuple-element.16), channel_id=1, source_target_pairs={{0,8},{8,0},{16,24},{24,16},{32,40},{40,32},{48,56},{56,48},{1,9},... | collective-permute-start | bytes 196616 | tf_op jit(solution)/shard_map/ppermute | solution.py:30
  18.8 23.6 %collective-permute-start.2 = (bf16[4,8192]{1,0:T(4,128)(2,1)S(1)}, bf16[4,8192]{1,0:T(4,128)(2,1)S(1)}, u32[]{:S(2)}, u32[]{:S(2)}) collective-permute-start(bf16[4,8192]{1,0:T(4,128)(2,1)S(1)} %get-tuple-element.17), channel_id=1, source_target_pairs={{0,16},{8,24},{16,0},{24,8},{32,48},{40,56},{48,32},{56,40},{1,17}... | collective-permute-start | bytes 196616 | tf_op jit(solution)/shard_map/ppermute | solution.py:30
  21.4 21.1 %collective-permute-start.3 = (bf16[4,8192]{1,0:T(4,128)(2,1)S(1)}, bf16[4,8192]{1,0:T(4,128)(2,1)S(1)}, u32[]{:S(2)}, u32[]{:S(2)}) collective-permute-start(bf16[4,8192]{1,0:T(4,128)(2,1)S(1)} %get-tuple-element.18), channel_id=1, source_target_pairs={{0,32},{8,40},{16,48},{24,56},{32,0},{40,8},{48,16},{56,24},{1,33}... | collective-permute-start | bytes 196616 | tf_op jit(solution)/shard_map/ppermute | solution.py:30
  29.3 13.1 %collective-permute-start.4 = (bf16[4,8192]{1,0:T(4,128)(2,1)S(1)}, bf16[4,8192]{1,0:T(4,128)(2,1)S(1)}, u32[]{:S(2)}, u32[]{:S(2)}) collective-permute-start(bf16[4,8192]{1,0:T(4,128)(2,1)S(1)} %get-tuple-element.19), channel_id=1, source_target_pairs={{0,64},{64,0},{128,192},{192,128},{256,320},{320,256},{384,448},{4... | collective-permute-start | bytes 196616 | tf_op jit(solution)/shard_map/ppermute | solution.py:30
  32.6 9.9 %collective-permute-start.5 = (bf16[4,8192]{1,0:T(4,128)(2,1)S(1)}, bf16[4,8192]{1,0:T(4,128)(2,1)S(1)}, u32[]{:S(2)}, u32[]{:S(2)}) collective-permute-start(bf16[4,8192]{1,0:T(4,128)(2,1)S(1)} %get-tuple-element.20), channel_id=1, source_target_pairs={{0,128},{64,192},{128,0},{192,64},{256,384},{320,448},{384,256},{4... | collective-permute-start | bytes 196616 | tf_op jit(solution)/shard_map/ppermute | solution.py:30
  36.8 9.0 %collective-permute-start.6 = (bf16[4,8192]{1,0:T(4,128)(2,1)S(1)}, bf16[4,8192]{1,0:T(4,128)(2,1)S(1)}, u32[]{:S(2)}, u32[]{:S(2)}) collective-permute-start(bf16[4,8192]{1,0:T(4,128)(2,1)S(1)} %get-tuple-element.21), channel_id=1, source_target_pairs={{0,256},{64,320},{128,384},{192,448},{256,0},{320,64},{384,128},{4... | collective-permute-start | bytes 196616 | tf_op jit(solution)/shard_map/ppermute | solution.py:30
  49.4 20.7 %all-to-all-start = ((s16[8,448,128]{2,1,0:T(8,128)(2,1)}), s16[8,448,128]{2,1,0:T(8,128)(2,1)}, u32[]{:S(2)}, u32[]{:S(2)}) async-start(s16[8,448,128]{2,1,0:T(8,128)(2,1)} %add_add_fusion), calls=%async_computation | async-start | bytes 1835008 | tf_op jit(solution)/shard_map/all_to_all | solution.py:52
  56.4 32.3 %copy-start.2 = (s32[1,512]{1,0:T(1,128)S(1)}, s32[1,512]{1,0:T(1,128)}, u32[]{:S(2)}) copy-start(s32[1,512]{1,0:T(1,128)} %param.8) | copy-start | bytes 6148
  84.3 12.2 %all-to-all-start.2 = ((s16[8,64,128]{2,1,0:T(8,128)(2,1)}), s16[8,64,128]{2,1,0:T(8,128)(2,1)S(1)}, u32[]{:S(2)}, u32[]{:S(2)}) async-start(s16[8,64,128]{2,1,0:T(8,128)(2,1)} %broadcast_in_dim.78), calls=%async_computation.2 | async-start | bytes 262144 | tf_op jit(solution)/shard_map/all_to_all | solution.py:52
  97.5 11.3 %all-to-all-start.3 = ((s16[8,64,128]{2,1,0:T(8,128)(2,1)}), s16[8,64,128]{2,1,0:T(8,128)(2,1)S(1)}, u32[]{:S(2)}, u32[]{:S(2)}) async-start(s16[8,64,128]{2,1,0:T(8,128)(2,1)} %broadcast_in_dim.79), calls=%async_computation.3 | async-start | bytes 262144 | tf_op jit(solution)/shard_map/all_to_all | solution.py:52
  110.1 21.1 %all-to-all-start.4 = ((s16[8,448,128]{2,1,0:T(8,128)(2,1)}), s16[8,448,128]{2,1,0:T(8,128)(2,1)S(1)}, u32[]{:S(2)}, u32[]{:S(2)}) async-start(s16[8,448,128]{2,1,0:T(8,128)(2,1)} %broadcast_in_dim.81), calls=%async_computation.4 | async-start | bytes 1835008 | tf_op jit(solution)/shard_map/all_to_all | solution.py:52

commit v3 on v2

--- a/solution.py
+++ b/solution.py
@@ -10,10 +10,7 @@
 
 
 SPACE = ("y", "z", "core")
-FULL = 16383.0
 FULL_BITS = 14
-SHARD_ROWS = 64
-SPARE = 16
 
 
 def bit_axes(sizes):
@@ -30,50 +27,107 @@
     return lax.ppermute(value, axis, pairs)
 
 
-def encode(values, extra=None):
-    rows = values.shape[-2]
-    peak = jnp.max(jnp.abs(values), axis=-2, keepdims=True)
+def encoded(values, rows, weight=None):
+    have = values.shape[0]
+    peak = jnp.max(jnp.abs(values), axis=0, keepdims=True)
     power = jnp.clip(jnp.ceil(jnp.log2(jnp.maximum(peak, 1e-30))), -100.0, 100.0)
-    coded = jnp.round(values * jnp.exp2(FULL_BITS - power)).astype(jnp.int16)
-    spare = [power.astype(jnp.int16)]
-    if extra is not None:
-        spare.append(jnp.broadcast_to(extra.astype(jnp.int16), power.shape))
-    fill = -rows % SPARE or SPARE
-    spare.append(jnp.zeros(values.shape[:-2] + (fill - len(spare), values.shape[-1]), jnp.int16))
-    return jnp.concatenate([coded] + spare, axis=-2)
-
-
-def decode(coded, rows):
-    power = coded[..., rows : rows + 1, :].astype(jnp.float32)
-    return coded[..., :rows, :].astype(jnp.float32) * jnp.exp2(power - FULL_BITS)
+    coded = jnp.round(values * jnp.exp2(FULL_BITS - power))
+    spare = (rows - have, values.shape[1])
+    place = lax.broadcasted_iota(jnp.int32, spare, 0)
+    extra = jnp.where(place == 0, jnp.broadcast_to(power, spare), 0.0)
+    if weight is not None:
+        extra = jnp.where(place == 1, weight, extra)
+    return jnp.concatenate([coded, extra], axis=0).astype(jnp.int32).astype(jnp.int16)
+
+
+def decoded(coded, have):
+    values = coded.astype(jnp.int32).astype(jnp.float32)
+    return values[:have] * jnp.exp2(values[have : have + 1] - FULL_BITS), values[have + 1 : have + 2]
+
+
+def near_kernel(have, copies, coded_ref, out_ref, total_ref):
+    summed = None
+    weights = None
+    for source in range(coded_ref.shape[0]):
+        values, weight = decoded(coded_ref[source], have)
+        values = values * weight
+        summed = values if summed is None else summed + values
+        weights = weight if weights is None else weights + weight
+    channels = summed.shape[1]
+    depth, rows, _ = out_ref.shape
+    step = rows - 8
+    summed = jnp.concatenate(
+        [summed, jnp.zeros((depth * step - have, channels), jnp.float32)], axis=0
+    )
+    for target in range(depth):
+        out_ref[target] = encoded(summed[target * step : (target + 1) * step], rows)
+    total_ref[...] = jnp.broadcast_to(weights * (1.0 / copies), total_ref.shape)
+
+
+def far_kernel(coded_ref, out_ref):
+    rows = coded_ref.shape[1]
+    summed = None
+    for source in range(coded_ref.shape[0]):
+        values, _ = decoded(coded_ref[source], rows - 8)
+        summed = values if summed is None else summed + values
+    code = encoded(summed, rows)
+    for target in range(out_ref.shape[0]):
+        out_ref[target] = code
+
+
+def joined_kernel(have, coded_ref, out_ref):
+    rows = coded_ref.shape[1]
+    parts = [decoded(coded_ref[source], rows - 8)[0] for source in range(coded_ref.shape[0])]
+    code = encoded(jnp.concatenate(parts, axis=0)[:have], out_ref.shape[1])
+    for target in range(out_ref.shape[0]):
+        out_ref[target] = code
+
+
+def final_kernel(have, scale, coded_ref, total_ref, out_ref):
+    factor = scale / total_ref[0:1, :]
+    for source in range(coded_ref.shape[0]):
+        values, _ = decoded(coded_ref[source], have)
+        out_ref[source * have : (source + 1) * have, :] = values * factor
 
 
 def exchanged(parts, axes):
     return lax.all_to_all(parts, axes, 0, 0, tiled=True)
 
 
-def everyone(part, axes, count):
-    return exchanged(jnp.broadcast_to(part[None], (count,) + part.shape), axes)
-
-
-def reduced(weighted, own_weight):
-    rows, channels = weighted.shape
+def reduced(coded, rows, scale):
+    near_count, near_rows, channels = coded.shape
+    have = rows // near_count
     near = ("core", "x")
-    near_count = lax.axis_size("core") * lax.axis_size("x")
     depth = lax.axis_size("z")
     breadth = lax.axis_size("y")
-    near_rows = rows // near_count
-    own_rows = near_rows // depth
-    parts = exchanged(encode(weighted.reshape(near_count, near_rows, channels), own_weight), near)
-    total_weight = jnp.sum(parts[:, near_rows + 1, 0].astype(jnp.float32)) / lax.axis_size("core")
-    part = jnp.sum(decode(parts, near_rows), axis=0)
-    parts = exchanged(encode(part.reshape(depth, own_rows, channels)), "z")
-    part = jnp.sum(decode(parts, own_rows), axis=0)
-    parts = everyone(encode(part), "y", breadth)
-    part = jnp.sum(decode(parts, own_rows), axis=0)
-    part = decode(everyone(encode(part), "z", depth), own_rows).reshape(near_rows, channels)
-    whole = decode(everyone(encode(part), near, near_count), near_rows).reshape(rows, channels)
-    return whole, total_weight
+    far_rows = -(-have // (8 * depth)) * 8 + 8
+    passed = jax.ShapeDtypeStruct((depth, far_rows, channels), jnp.int16)
+    spread = jax.ShapeDtypeStruct((breadth, far_rows, channels), jnp.int16)
+    part, total = local_call(
+        functools.partial(near_kernel, have, lax.axis_size("core")),
+        [passed, jax.ShapeDtypeStruct((8, channels), jnp.float32)],
+        [],
+        rows * channels * 4,
+        2 * rows * channels,
+    )(exchanged(coded, near))
+    small = depth * far_rows * channels
+    part = local_call(far_kernel, spread, [], small, 2 * small)(exchanged(part, "z"))
+    part = local_call(far_kernel, passed, [], small, 2 * small)(exchanged(part, "y"))
+    whole = local_call(
+        functools.partial(joined_kernel, have),
+        jax.ShapeDtypeStruct(coded.shape, jnp.int16),
+        [],
+        small,
+        2 * rows * channels,
+    )(exchanged(part, "z"))
+    result = local_call(
+        functools.partial(final_kernel, have, scale),
+        jax.ShapeDtypeStruct((rows, channels), jnp.float32),
+        [],
+        rows * channels * 4,
+        6 * rows * channels,
+    )(exchanged(whole, near), total)
+    return result, total
 
 
 def halo_place(pair_table, device, bricks, nspace, peer_cap, levels):
@@ -101,6 +155,12 @@
 
 def onehot(left, right, dtype=jnp.bfloat16):
     return jnp.where(left == right, 1.0, 0.0).astype(dtype)
+
+
+def voxel_rows(natural_ref, bricks):
+    return [
+        natural_ref[pl.ds(voxel, bricks, stride=64), :] for voxel in range(64)
+    ]
 
 
 def stacked_rows(rows):
@@ -115,13 +175,26 @@
     )
 
 
-def backward_kernel(levels, grad_ref, own_ref, kernel_ref, rows_ref, pick_ref, *refs):
+def backward_kernel(
+    levels, feature_ref, cotangent_ref, mask_ref, kernel_ref, rows_ref, pick_ref, *refs
+):
     send_refs = refs[:levels]
-    own_grad_ref, cube_ref, table_ref = refs[levels:]
-    bricks = grad_ref.shape[0]
+    own_grad_ref, own_ref, grad_ref, cube_ref, table_ref, natural_ref = refs[levels:]
+    bricks = mask_ref.shape[0]
     channels = kernel_ref.shape[1]
     wide = 4 * channels
-    grad = grad_ref[...].astype(jnp.float32)
+    masks = [
+        jnp.broadcast_to(mask_ref[:, voxel : voxel + 1], (bricks, channels)) for voxel in range(64)
+    ]
+    natural_ref[0] = cotangent_ref[...].astype(jnp.float32)
+    natural_ref[1] = feature_ref[...].astype(jnp.float32)
+    grads = [
+        rows * mask for rows, mask in zip(voxel_rows(natural_ref.at[0], bricks), masks)
+    ]
+    owns = [rows * mask for rows, mask in zip(voxel_rows(natural_ref.at[1], bricks), masks)]
+    grad = jnp.concatenate(grads, axis=1)
+    grad_ref[...] = grad.astype(jnp.bfloat16)
+    own_ref[...] = jnp.concatenate(owns, axis=1).astype(jnp.bfloat16)
     stacked = stacked_rows(grad).astype(jnp.bfloat16)
     cube_ref[...] = jnp.zeros_like(cube_ref)
     for tap in range(9):
@@ -185,7 +258,7 @@
         own_grad_ref[:, span] = table_ref[pick_rows:, span] + grad[:, span]
 
 
-def patch_kernel(table_ref, grad_ref, rows_ref, weight_ref, cube_ref):
+def patch_kernel(table_ref, grad_ref, rows_ref, scan_ref, code_ref, cube_ref, weight_ref):
     bricks = grad_ref.shape[0]
     table_rows = table_ref.shape[0]
     channels = weight_ref.shape[1]
@@ -226,6 +299,13 @@
         for tap_z in range(3):
             row = (tap * 3 + tap_z) * channels
             weight_ref[row : row + channels, :] = part[:, tap_z * channels : (tap_z + 1) * channels].T
+    own_weight = scan_ref[0].astype(jnp.float32)
+    near_count, near_rows, _ = code_ref.shape
+    have = weight_ref.shape[0] // near_count
+    for target in range(near_count):
+        code_ref[target] = encoded(
+            weight_ref[target * have : (target + 1) * have, :], near_rows, own_weight
+        )
 
 
 def columns_of(cube_ref, tap):
@@ -240,7 +320,19 @@
 
 
 def forward_kernel(
-    cube_ref, kernel_ref, table_ref, own_ref, own_grad_ref, back_ref, mask_ref, out_ref, sum_ref
+    scans,
+    cube_ref,
+    kernel_ref,
+    table_ref,
+    own_ref,
+    own_grad_ref,
+    back_ref,
+    mask_ref,
+    scan_ref,
+    total_ref,
+    out_ref,
+    sum_ref,
+    natural_ref,
 ):
     bricks = own_ref.shape[0]
     channels = kernel_ref.shape[1]
@@ -254,22 +346,35 @@
         total = part if total is None else total + part
     owners = lax.broadcasted_iota(jnp.int32, (bricks, table_ref.shape[0]), 0)
     backer = onehot(owners, jnp.broadcast_to(back_ref[...], owners.shape))
+    factor = jnp.broadcast_to(
+        scan_ref[0].astype(jnp.float32) * scans / total_ref[0:1, :], (bricks, channels)
+    )
     for xy in range(16):
+        back = jnp.dot(
+            backer,
+            table_ref[:, xy * 4 * channels : (xy + 1) * 4 * channels],
+            preferred_element_type=jnp.float32,
+        )
         for z in range(4):
             voxel = xy * 4 + z
             span = slice(voxel * channels, (voxel + 1) * channels)
             row = (z * 16 + xy) * bricks
             mask = jnp.broadcast_to(mask_ref[:, voxel : voxel + 1], (bricks, channels))
             own = own_ref[:, span].astype(jnp.float32)
-            out_ref[:, span] = (mask * (total[row : row + bricks] + own)).astype(jnp.bfloat16)
-            back = jnp.dot(backer, table_ref[:, span], preferred_element_type=jnp.float32)
-            sum_ref[:, span] = mask * (own_grad_ref[:, span] + back)
-
-
-def local_call(body, out_shape, scratch, flops, moved):
+            lines = pl.ds(voxel, bricks, stride=64)
+            natural_ref[0, lines, :] = mask * (total[row : row + bricks] + own)
+            grads = own_grad_ref[:, span] + back[:, z * channels : (z + 1) * channels]
+            natural_ref[1, lines, :] = factor * (mask * grads)
+    out_ref[...] = natural_ref[0].astype(jnp.bfloat16)
+    sum_ref[...] = natural_ref[1].astype(jnp.bfloat16)
+
+
+def local_call(body, out_shape, scratch, flops, moved, in_specs=None):
+    keys = {} if in_specs is None else {"in_specs": in_specs}
     return pl.pallas_call(
         body,
         out_shape=out_shape,
+        **keys,
         scratch_shapes=scratch,
         compiler_params=pltpu.CompilerParams(vmem_limit_bytes=40 * 1024 * 1024),
         cost_estimate=pl.CostEstimate(flops=flops, bytes_accessed=moved, transcendentals=0),
@@ -291,9 +396,6 @@
     send_rows = -(-4 * levels // 8) * 8
     table_rows = send_rows + bricks
     width = 64 * channels
-    voxel_mask = occupancy[0][:, None].astype(jnp.bfloat16)
-    masked = (features[0] * voxel_mask).reshape(bricks, width)
-    grad_in = (cotangent[0] * voxel_mask).reshape(bricks, width)
     mask_float = occupancy[0].reshape(bricks, 64).astype(jnp.float32)
     kind, level_of, within = halo_place(brick_pairs[0].T, device, bricks, nspace, peer_cap, levels)
     pair_table = brick_pairs[0].T
@@ -319,47 +421,46 @@
     ).reshape(1, table_rows)
     macs = own_rows * 27 * channels * channels
     cube = (36, bricks, 6 * channels)
-    *sends, own_grad = local_call(
+    rowed = jax.ShapeDtypeStruct((bricks, width), jnp.bfloat16)
+    plain = jax.ShapeDtypeStruct((own_rows, channels), jnp.bfloat16)
+    natural = pltpu.VMEM((2, own_rows, channels), jnp.float32)
+    *sends, own_grad, masked, grad_in = local_call(
         functools.partial(backward_kernel, levels),
         [jax.ShapeDtypeStruct((4, width), jnp.bfloat16)] * levels
-        + [jax.ShapeDtypeStruct((bricks, width), jnp.float32)],
-        [pltpu.VMEM(cube, jnp.float32), pltpu.VMEM((table_rows, width), jnp.float32)],
+        + [jax.ShapeDtypeStruct((bricks, width), jnp.float32), rowed, rowed],
+        [pltpu.VMEM(cube, jnp.float32), pltpu.VMEM((table_rows, width), jnp.float32), natural],
         2 * macs,
         4 * 2**20,
-    )(grad_in, masked, kernel, backward_rows, pick_rows)
+    )(features[0], cotangent[0], mask_float, kernel, backward_rows, pick_rows)
     came = [swapped(sends[level], steps[level]) for level in range(levels)]
     blank = jnp.zeros((send_rows - 4 * levels, width), jnp.bfloat16)
     table = jnp.concatenate(came + [blank, masked], axis=0)
-    weight_grad, cubes = local_call(
+    near_count = lax.axis_size("core") * lax.axis_size("x")
+    near_rows = kernel.shape[0] // near_count + 16
+    scalar = pl.BlockSpec(memory_space=pltpu.SMEM)
+    whole = pl.BlockSpec(memory_space=pltpu.VMEM)
+    coded, cubes = local_call(
         patch_kernel,
         [
-            jax.ShapeDtypeStruct(kernel.shape, jnp.float32),
+            jax.ShapeDtypeStruct((near_count, near_rows, channels), jnp.int16),
             jax.ShapeDtypeStruct(cube, jnp.float32),
         ],
-        [],
+        [pltpu.VMEM(kernel.shape, jnp.float32)],
         2 * macs,
         4 * 2**20,
-    )(table, grad_in, forward_rows)
-    output, grad_sum = local_call(
-        forward_kernel,
-        [
-            jax.ShapeDtypeStruct((bricks, width), jnp.bfloat16),
-            jax.ShapeDtypeStruct((bricks, width), jnp.float32),
-        ],
-        [],
+        [whole] * 3 + [scalar],
+    )(table, grad_in, forward_rows, scan_weight)
+    scale = scan_count / math.sqrt(64.0 * bricks * nspace)
+    kernel_grad, weight_total = reduced(coded, kernel.shape[0], scale)
+    output, grad_features = local_call(
+        functools.partial(forward_kernel, float(scan_count)),
+        [plain, plain],
+        [natural],
         2 * macs,
         4 * 2**20,
-    )(cubes, kernel, table, masked, own_grad, back_rows, mask_float)
-    own_weight = scan_weight[0].astype(jnp.float32)
-    summed, weight_total = reduced(weight_grad * own_weight, own_weight)
-    factor = own_weight * scan_count / weight_total
-    grad_features = (factor * grad_sum).astype(jnp.bfloat16)
-    kernel_grad = summed * (scan_count / weight_total) / math.sqrt(64.0 * bricks * nspace)
-    return (
-        output.reshape(1, own_rows, channels),
-        grad_features.reshape(1, own_rows, channels),
-        kernel_grad,
-    )
+        [whole] * 7 + [scalar, whole],
+    )(cubes, kernel, table, masked, own_grad, back_rows, mask_float, scan_weight, weight_total)
+    return (output[None], grad_features[None], kernel_grad)
 
 
 def solution(mesh):

time: 134 us -> 128 us (0.955)
  blocking collectives: 10.8 us -> 53.8 us
  waiting for transfers between devices: 41.2 us -> 14 us
  starting transfers between devices: 55.6 us -> 40.9 us
  other arithmetic: 8.29 us -> 0.99 us
  Pallas kernels: 4.87 us -> 9.11 us
  local copies, waits for them, and re-layouts: 9.65 us -> 7.1 us
    all_to_all x1 -> x4, blocking collectives: 10.8 us -> 53.8 us  [exchanged(): return lax.all_to_all(parts, axes, 0, 0, tiled=True)]
    all_to_all x4 -> x1, waiting for transfers between devices: 37.9 us -> 10.5 us  [exchanged(): return lax.all_to_all(parts, axes, 0, 0, tiled=True)]
    all_to_all x4 -> x1, starting transfers between devices: 22.2 us -> 7.57 us  [exchanged(): return lax.all_to_all(parts, axes, 0, 0, tiled=True)]
    unnamed x7 -> x15, local copies, waits for them, and re-layouts: 0.79 us -> 5.4 us
    pallas_call x2 -> x7, Pallas kernels: 2.6 us -> 6.64 us  [the longest x1 2.06 us: on_device(): local_call(functools.partial(forward_kernel, float(scan_count)), [plain,...]
    reduce_sum x4 -> x0, other arithmetic: 2.98 us -> none  [the longest x1 1.54 us: reduced(): part = jnp.sum(decode(parts, near_rows), axis=0)]
    broadcast_in_dim x6 -> x0, local copies, waits for them, and re-layouts: 2.41 us -> none  [the longest x3 2.4 us: everyone(): return exchanged(jnp.broadcast_to(part[None], (count,) + part.shape), axes)]
    squeeze x2 -> x0, local copies, waits for them, and re-layouts: 2.01 us -> none  [the longest x1 1.04 us: on_device(): masked = (features[0] * voxel_mask).reshape(bricks, width)]
  transfers between devices with their start and end apart: 11 -> 8, of which waited for: 5 -> 2; matrix products, arithmetic and copies ran while one was open for 3% -> 0% of each run, Pallas kernels for 1% -> 2%
where the time goes in v3:
time: 128 us; the launch traced here: 127 us
  blocking collectives  53.8 us (42%)
  starting transfers between devices  40.9 us (32%)
  waiting for transfers between devices  14 us (11%)
  Pallas kernels  9.11 us (7%)
  local copies, waits for them, and re-layouts  7.1 us (6%)
  between operations  1.49 us (1%)
    all_to_all x4, blocking collectives, exchanged(): return lax.all_to_all(parts, axes, 0, 0, tiled=True)  53.8 us
    ppermute x7, starting transfers between devices, swapped(): return lax.ppermute(value, axis, pairs)  33.3 us
    all_to_all x1, waiting for transfers between devices, exchanged(): return lax.all_to_all(parts, axes, 0, 0, tiled=True)  10.5 us
    all_to_all x1, starting transfers between devices, exchanged(): return lax.all_to_all(parts, axes, 0, 0, tiled=True)  7.57 us
    unnamed x15, local copies, waits for them, and re-layouts  5.4 us
    ppermute x7, waiting for transfers between devices, swapped(): return lax.ppermute(value, axis, pairs)  3.48 us
  transfers between devices with their start and end apart: 8, of which 2 were waited for; matrix products, arithmetic and copies ran while one was open for 0% of the time, Pallas kernels for 2%

profile of v3, /device:TPU:1, one launch (start us, length us, event | category | flops | bytes accessed | tf_op | source)
XLA Modules:
  0.0 127.4 jit_solution(13542993387548711013)
XLA Ops:
  2.7 0.8 copy.15
  3.6 1.2 copy-done.1
  4.8 0.9 copy-done.5
  5.7 0.9 copy-done.6
  6.6 2.5 %shard_map.94 = (bf16[4,8192]{1,0:T(4,128)(2,1)S(1)}, bf16[4,8192]{1,0:T(4,128)(2,1)S(1)}, bf16[4,8192]{1,0:T(4,128)(2,1)S(1)}, bf16[4,8192]{1,0:T(4,128)(2,1)S(...) custom-call(bf16[512,128]{1,0:T(8,128)(2,1)S(1)} %bitcast.54, ...), custom_call_target="tpu_custom_call" | custom-call | flops 452984832 | bytes 4194304 | tf_op jit(solution)/shard_map/pallas_call | solution.py:427
  9.7 8.7 %collective-permute-start = (bf16[4,8192]{1,0:T(4,128)(2,1)S(1)}, bf16[4,8192]{1,0:T(4,128)(2,1)S(1)}, u32[]{:S(2)}, u32[]{:S(2)}) collective-permute-start(bf16[4,8192]{1,0:T(4,128)(2,1)S(1)} %get-tuple-element.19), channel_id=1, source_target_pairs={{0,4},{4,0},{1,5},{5,1},{2,6},{6,2},{3,7},{7,3},{8,12},{12,8},{9,1... | collective-permute-start | bytes 196616 | tf_op jit(solution)/shard_map/ppermute | solution.py:27
  18.5 1.9 %collective-permute-start.1 = (bf16[4,8192]{1,0:T(4,128)(2,1)S(1)}, bf16[4,8192]{1,0:T(4,128)(2,1)S(1)}, u32[]{:S(2)}, u32[]{:S(2)}) collective-permute-start(bf16[4,8192]{1,0:T(4,128)(2,1)S(1)} %get-tuple-element.20), channel_id=1, source_target_pairs={{0,8},{8,0},{16,24},{24,16},{32,40},{40,32},{48,56},{56,48},{1,9},... | collective-permute-start | bytes 196616 | tf_op jit(solution)/shard_map/ppermute | solution.py:27
  20.4 2.5 %collective-permute-start.2 = (bf16[4,8192]{1,0:T(4,128)(2,1)S(1)}, bf16[4,8192]{1,0:T(4,128)(2,1)S(1)}, u32[]{:S(2)}, u32[]{:S(2)}) collective-permute-start(bf16[4,8192]{1,0:T(4,128)(2,1)S(1)} %get-tuple-element.21), channel_id=1, source_target_pairs={{0,16},{8,24},{16,0},{24,8},{32,48},{40,56},{48,32},{56,40},{1,17}... | collective-permute-start | bytes 196616 | tf_op jit(solution)/shard_map/ppermute | solution.py:27
  23.0 7.9 %collective-permute-start.3 = (bf16[4,8192]{1,0:T(4,128)(2,1)S(1)}, bf16[4,8192]{1,0:T(4,128)(2,1)S(1)}, u32[]{:S(2)}, u32[]{:S(2)}) collective-permute-start(bf16[4,8192]{1,0:T(4,128)(2,1)S(1)} %get-tuple-element.22), channel_id=1, source_target_pairs={{0,32},{8,40},{16,48},{24,56},{32,0},{40,8},{48,16},{56,24},{1,33}... | collective-permute-start | bytes 196616 | tf_op jit(solution)/shard_map/ppermute | solution.py:27
  30.9 3.2 %collective-permute-start.4 = (bf16[4,8192]{1,0:T(4,128)(2,1)S(1)}, bf16[4,8192]{1,0:T(4,128)(2,1)S(1)}, u32[]{:S(2)}, u32[]{:S(2)}) collective-permute-start(bf16[4,8192]{1,0:T(4,128)(2,1)S(1)} %get-tuple-element.23), channel_id=1, source_target_pairs={{0,64},{64,0},{128,192},{192,128},{256,320},{320,256},{384,448},{4... | collective-permute-start | bytes 196616 | tf_op jit(solution)/shard_map/ppermute | solution.py:27
  34.1 4.2 %collective-permute-start.5 = (bf16[4,8192]{1,0:T(4,128)(2,1)S(1)}, bf16[4,8192]{1,0:T(4,128)(2,1)S(1)}, u32[]{:S(2)}, u32[]{:S(2)}) collective-permute-start(bf16[4,8192]{1,0:T(4,128)(2,1)S(1)} %get-tuple-element.24), channel_id=1, source_target_pairs={{0,128},{64,192},{128,0},{192,64},{256,384},{320,448},{384,256},{4... | collective-permute-start | bytes 196616 | tf_op jit(solution)/shard_map/ppermute | solution.py:27
  38.4 4.8 %collective-permute-start.6 = (bf16[4,8192]{1,0:T(4,128)(2,1)S(1)}, bf16[4,8192]{1,0:T(4,128)(2,1)S(1)}, u32[]{:S(2)}, u32[]{:S(2)}) collective-permute-start(bf16[4,8192]{1,0:T(4,128)(2,1)S(1)} %get-tuple-element.25), channel_id=1, source_target_pairs={{0,256},{64,320},{128,384},{192,448},{256,0},{320,64},{384,128},{4... | collective-permute-start | bytes 196616 | tf_op jit(solution)/shard_map/ppermute | solution.py:27
  43.9 3.5 %collective-permute-done.6 = bf16[4,8192]{1,0:T(4,128)(2,1)S(1)} collective-permute-done((bf16[4,8192]{1,0:T(4,128)(2,1)S(1)}, bf16[4,8192]{1,0:T(4,128)(2,1)S(1)}, u32[]{:S(2)}, u32[]{:S(2)}) %collective-permute-start.6) | collective-permute-done | bytes 65568 | tf_op jit(solution)/shard_map/ppermute | solution.py:27
  47.8 1.5 %shard_map.95 = (s16[8,448,128]{2,1,0:T(8,128)(2,1)S(1)}, f32[36,8,768]{2,1,0:T(8,128)S(1)}) custom-call(bf16[40,8192]{1,0:T(8,128)(2,1)S(1)} %concatenate.14.table_ref, bf16[8,8192]{1,0:T(8,128)(2,1)S(1)} %get-tuple-element.27.grad_ref, s32[216,1]{1,0:T(8,128)S(1)} %reshape.102.rows_ref, s32[1]{0:T(128)S(6)} %copy.21.scan_ref), custom_call_target="tpu_custom_call" | custom-call | flops 452984832 | bytes 4194304 | tf_op jit(solution)/shard_map/pallas_call | solution.py:442
  49.3 20.5 %all_to_all.25.coded_ref = s16[8,448,128]{2,1,0:T(8,128)(2,1)S(1)} all-to-all(s16[8,448,128]{2,1,0:T(8,128)(2,1)S(1)} %get-tuple-element.30), channel_id=1, replica_groups=mesh['y'=8,'z'=8,'core'=2,'x'=4] {'core','x'}, dimensions={0} | all-to-all | bytes 1835008 | tf_op jit(solution)/shard_map/all_to_all | solution.py:94
  70.2 10.7 %all_to_all.26.coded_ref = s16[8,64,128]{2,1,0:T(8,128)(2,1)S(1)} all-to-all(s16[8,64,128]{2,1,0:T(8,128)(2,1)S(1)} %get-tuple-element.34), channel_id=1, replica_groups=mesh['y'=8,'z'=8,'core'=2,'x'=4] {'z'}, dimensions={0} | all-to-all | bytes 262144 | tf_op jit(solution)/shard_map/all_to_all | solution.py:94
  80.9 12.1 %all_to_all.27.coded_ref = s16[8,64,128]{2,1,0:T(8,128)(2,1)S(1)} all-to-all(s16[8,64,128]{2,1,0:T(8,128)(2,1)S(1)} %shard_map.98), channel_id=1, replica_groups=mesh['y'=8,'z'=8,'core'=2,'x'=4] {'y'}, dimensions={0} | all-to-all | bytes 262144 | tf_op jit(solution)/shard_map/all_to_all | solution.py:94
  93.1 10.5 %all_to_all.28.coded_ref = s16[8,64,128]{2,1,0:T(8,128)(2,1)S(1)} all-to-all(s16[8,64,128]{2,1,0:T(8,128)(2,1)S(1)} %shard_map.99), channel_id=1, replica_groups=mesh['y'=8,'z'=8,'core'=2,'x'=4] {'z'}, dimensions={0} | all-to-all | bytes 262144 | tf_op jit(solution)/shard_map/all_to_all | solution.py:94
  103.7 1.1 shard_map.100
  104.8 7.6 %all-to-all-start.4 = ((s16[8,448,128]{2,1,0:T(8,128)(2,1)}), s16[8,448,128]{2,1,0:T(8,128)(2,1)S(1)}, u32[]{:S(2)}, u32[]{:S(2)}) async-start(s16[8,448,128]{2,1,0:T(8,128)(2,1)} %shard_map.100), calls=%async_computation.4 | async-start | bytes 1835008 | tf_op jit(solution)/shard_map/all_to_all | solution.py:94
  112.4 0.9 copy-done.4
  113.4 2.1 %shard_map.97 = (bf16[512,128]{1,0:T(8,128)(2,1)}, bf16[512,128]{1,0:T(8,128)(2,1)}) custom-call(f32[36,8,768]{2,1,0:T(8,128)S(1)} %get-tuple-element.28.cube_ref, bf16[3456,128]{1,0:T(8,128)(2,1)S(1)} %copy-done.2, bf16[40,8192]{1,0:T(8,128)(2,1)S(1)} %concatenate.14.table_ref, bf16[8,8192]{1,0:T(8,128)(2,1)S(1)} %get-tuple-element.26.own_ref, ...), custom_call_target="tpu_custom_call" | custom-call | flops 452984832 | bytes 4194304 | tf_op jit(solution)/shard_map/pallas_call | solution.py:455
  115.4 10.5 %all-to-all-done.4.coded_ref = s16[8,448,128]{2,1,0:T(8,128)(2,1)S(1)} async-done(((s16[8,448,128]{2,1,0:T(8,128)(2,1)}), s16[8,448,128]{2,1,0:T(8,128)(2,1)S(1)}, u32[]{:S(2)}, u32[]{:S(2)}) %all-to-all-start.4) | async-done | bytes 917536 | tf_op jit(solution)/shard_map/all_to_all | solution.py:94
  125.9 1.4 %shard_map.101 = f32[3456,128]{1,0:T(8,128)} custom-call(s16[8,448,128]{2,1,0:T(8,128)(2,1)S(1)} %all-to-all-done.4.coded_ref, f32[8,128]{1,0:T(8,128)S(1)} %get-tuple-element.31.total_ref), custom_call_target="tpu_custom_call" | custom-call | flops 1769472 | bytes 2654208 | tf_op jit(solution)/shard_map/pallas_call | solution.py:123
  (40 shorter events, 3.9 us)
Async XLA Ops:
  0.6 1.0 copy-start
  3.6 1.2 copy-start.1
  4.8 0.9 copy-start.5
  5.7 0.9 copy-start.6
  9.1 0.7 copy-start.3
  9.7 24.4 %collective-permute-start = (bf16[4,8192]{1,0:T(4,128)(2,1)S(1)}, bf16[4,8192]{1,0:T(4,128)(2,1)S(1)}, u32[]{:S(2)}, u32[]{:S(2)}) collective-permute-start(bf16[4,8192]{1,0:T(4,128)(2,1)S(1)} %get-tuple-element.19), channel_id=1, source_target_pairs={{0,4},{4,0},{1,5},{5,1},{2,6},{6,2},{3,7},{7,3},{8,12},{12,8},{9,1... | collective-permute-start | bytes 196616 | tf_op jit(solution)/shard_map/ppermute | solution.py:27
  18.5 19.9 %collective-permute-start.1 = (bf16[4,8192]{1,0:T(4,128)(2,1)S(1)}, bf16[4,8192]{1,0:T(4,128)(2,1)S(1)}, u32[]{:S(2)}, u32[]{:S(2)}) collective-permute-start(bf16[4,8192]{1,0:T(4,128)(2,1)S(1)} %get-tuple-element.20), channel_id=1, source_target_pairs={{0,8},{8,0},{16,24},{24,16},{32,40},{40,32},{48,56},{56,48},{1,9},... | collective-permute-start | bytes 196616 | tf_op jit(solution)/shard_map/ppermute | solution.py:27
  20.4 23.5 %collective-permute-start.2 = (bf16[4,8192]{1,0:T(4,128)(2,1)S(1)}, bf16[4,8192]{1,0:T(4,128)(2,1)S(1)}, u32[]{:S(2)}, u32[]{:S(2)}) collective-permute-start(bf16[4,8192]{1,0:T(4,128)(2,1)S(1)} %get-tuple-element.21), channel_id=1, source_target_pairs={{0,16},{8,24},{16,0},{24,8},{32,48},{40,56},{48,32},{56,40},{1,17}... | collective-permute-start | bytes 196616 | tf_op jit(solution)/shard_map/ppermute | solution.py:27
  23.0 20.9 %collective-permute-start.3 = (bf16[4,8192]{1,0:T(4,128)(2,1)S(1)}, bf16[4,8192]{1,0:T(4,128)(2,1)S(1)}, u32[]{:S(2)}, u32[]{:S(2)}) collective-permute-start(bf16[4,8192]{1,0:T(4,128)(2,1)S(1)} %get-tuple-element.22), channel_id=1, source_target_pairs={{0,32},{8,40},{16,48},{24,56},{32,0},{40,8},{48,16},{56,24},{1,33}... | collective-permute-start | bytes 196616 | tf_op jit(solution)/shard_map/ppermute | solution.py:27
  30.9 13.0 %collective-permute-start.4 = (bf16[4,8192]{1,0:T(4,128)(2,1)S(1)}, bf16[4,8192]{1,0:T(4,128)(2,1)S(1)}, u32[]{:S(2)}, u32[]{:S(2)}) collective-permute-start(bf16[4,8192]{1,0:T(4,128)(2,1)S(1)} %get-tuple-element.23), channel_id=1, source_target_pairs={{0,64},{64,0},{128,192},{192,128},{256,320},{320,256},{384,448},{4... | collective-permute-start | bytes 196616 | tf_op jit(solution)/shard_map/ppermute | solution.py:27
  34.1 9.8 %collective-permute-start.5 = (bf16[4,8192]{1,0:T(4,128)(2,1)S(1)}, bf16[4,8192]{1,0:T(4,128)(2,1)S(1)}, u32[]{:S(2)}, u32[]{:S(2)}) collective-permute-start(bf16[4,8192]{1,0:T(4,128)(2,1)S(1)} %get-tuple-element.24), channel_id=1, source_target_pairs={{0,128},{64,192},{128,0},{192,64},{256,384},{320,448},{384,256},{4... | collective-permute-start | bytes 196616 | tf_op jit(solution)/shard_map/ppermute | solution.py:27
  38.4 9.0 %collective-permute-start.6 = (bf16[4,8192]{1,0:T(4,128)(2,1)S(1)}, bf16[4,8192]{1,0:T(4,128)(2,1)S(1)}, u32[]{:S(2)}, u32[]{:S(2)}) collective-permute-start(bf16[4,8192]{1,0:T(4,128)(2,1)S(1)} %get-tuple-element.25), channel_id=1, source_target_pairs={{0,256},{64,320},{128,384},{192,448},{256,0},{320,64},{384,128},{4... | collective-permute-start | bytes 196616 | tf_op jit(solution)/shard_map/ppermute | solution.py:27
  93.0 19.4 %copy-start.2 = (bf16[3456,128]{1,0:T(8,128)(2,1)S(1)}, bf16[3456,128]{1,0:T(8,128)(2,1)}, u32[]{:S(2)}) copy-start(bf16[3456,128]{1,0:T(8,128)(2,1)} %kernel_ref.3) | copy-start | bytes 2654212
  104.8 21.1 %all-to-all-start.4 = ((s16[8,448,128]{2,1,0:T(8,128)(2,1)}), s16[8,448,128]{2,1,0:T(8,128)(2,1)S(1)}, u32[]{:S(2)}, u32[]{:S(2)}) async-start(s16[8,448,128]{2,1,0:T(8,128)(2,1)} %shard_map.100), calls=%async_computation.4 | async-start | bytes 1835008 | tf_op jit(solution)/shard_map/all_to_all | solution.py:94
  112.4 1.0 copy-start.4

commit v4 on v3

--- a/solution.py
+++ b/solution.py
@@ -95,7 +95,7 @@
 
 
 def reduced(coded, rows, scale):
-    near_count, near_rows, channels = coded.shape
+    near_count, _, channels = coded.shape
     have = rows // near_count
     near = ("core", "x")
     depth = lax.axis_size("z")
@@ -132,14 +132,14 @@
 
 def halo_place(pair_table, device, bricks, nspace, peer_cap, levels):
     relative = jnp.clip(pair_table - bricks, 0, nspace * peer_cap - 1)
-    flipped = jnp.bitwise_xor(relative // peer_cap, device)
+    flipped = jnp.bitwise_xor(lax.div(relative, peer_cap), device)
     level_of = jnp.zeros_like(pair_table)
     for bit_level in range(levels):
         level_of = level_of + bit_level * (flipped == 1 << bit_level).astype(jnp.int32)
     kind = jnp.where(
         pair_table < bricks, 0, jnp.where(pair_table >= bricks + nspace * peer_cap, 2, 1)
     )
-    return kind, level_of, relative % peer_cap
+    return kind, level_of, lax.rem(relative, peer_cap)
 
 
 def voxel_sources():
@@ -176,15 +176,74 @@
 
 
 def backward_kernel(
-    levels, feature_ref, cotangent_ref, mask_ref, kernel_ref, rows_ref, pick_ref, *refs
+    levels,
+    peer_cap,
+    feature_hbm,
+    cotangent_hbm,
+    kernel_hbm,
+    occupancy_hbm,
+    pair_hbm,
+    send_hbm,
+    *refs,
 ):
     send_refs = refs[:levels]
-    own_grad_ref, own_ref, grad_ref, cube_ref, table_ref, natural_ref = refs[levels:]
+    own_grad_ref, own_ref, grad_ref, mask_ref, forward_ref, backer_ref = refs[levels : levels + 6]
+    cube_ref, table_ref, natural_ref, *staged, copy_sems = refs[levels + 6 :]
+    feature_ref, cotangent_ref, kernel_ref, occupancy_ref, pair_ref, list_ref = staged
+    sources = (feature_hbm, cotangent_hbm, kernel_hbm, occupancy_hbm, pair_hbm, send_hbm)
+    copies = [
+        pltpu.make_async_copy(source, target, copy_sems.at[at])
+        for at, (source, target) in enumerate(zip(sources, staged))
+    ]
+    for copy in copies:
+        copy.start()
+    cube_ref[...] = jnp.zeros_like(cube_ref)
     bricks = mask_ref.shape[0]
     channels = kernel_ref.shape[1]
     wide = 4 * channels
+    table_rows = table_ref.shape[0]
+    pick_rows = table_rows - bricks
+    for copy in copies:
+        copy.wait()
+    device = lax.axis_index(SPACE)
+    occupancy = occupancy_ref[...].astype(jnp.float32)
+    mask = jnp.concatenate(
+        [occupancy[:, 64 * brick : 64 * brick + 64] for brick in range(bricks)], axis=0
+    )
+    mask_ref[...] = mask
+    pairs = pair_ref[...]
+    kind, level_of, within = halo_place(
+        pairs, device, bricks, list_ref.shape[1] // peer_cap, peer_cap, levels
+    )
+    forward = jnp.where(
+        kind == 0, pick_rows + pairs, jnp.where(kind == 1, 4 * level_of + within, -1)
+    )
+    forward_ref[...] = forward
+    backward = jnp.where(kind == 1, forward + peer_cap, forward).astype(jnp.float32)
+    turned = jnp.concatenate(
+        [backward, jnp.zeros((bricks, 128 - backward.shape[1]), jnp.float32)], axis=1
+    ).T.astype(jnp.int32)
+    turned = jnp.concatenate([turned, turned], axis=1)
+    pick_row = lax.broadcasted_iota(jnp.int32, (pick_rows, bricks), 0)
+    pick_lane = lax.broadcasted_iota(jnp.int32, (pick_rows, bricks), 1)
+    back_row = lax.broadcasted_iota(jnp.int32, (bricks, table_rows), 0)
+    back_lane = lax.broadcasted_iota(jnp.int32, (bricks, table_rows), 1)
+    picker = jnp.zeros(pick_row.shape, jnp.float32)
+    backer = jnp.zeros(back_row.shape, jnp.float32)
+    for level in range(levels):
+        partner = jnp.bitwise_xor(device, 1 << level)
+        for entry in range(peer_cap):
+            chosen = list_ref[0, partner * peer_cap + entry]
+            at_pick = jnp.logical_and(pick_row == 4 * level + entry, pick_lane == chosen)
+            at_back = jnp.logical_and(
+                back_lane == 4 * level + peer_cap + entry, back_row == chosen
+            )
+            picker = jnp.where(at_pick, 1.0, picker)
+            backer = jnp.where(at_back, 1.0, backer)
+    picker = picker.astype(jnp.bfloat16)
+    backer_ref[...] = backer.astype(jnp.bfloat16)
     masks = [
-        jnp.broadcast_to(mask_ref[:, voxel : voxel + 1], (bricks, channels)) for voxel in range(64)
+        jnp.broadcast_to(mask[:, voxel : voxel + 1], (bricks, channels)) for voxel in range(64)
     ]
     natural_ref[0] = cotangent_ref[...].astype(jnp.float32)
     natural_ref[1] = feature_ref[...].astype(jnp.float32)
@@ -196,7 +255,6 @@
     grad_ref[...] = grad.astype(jnp.bfloat16)
     own_ref[...] = jnp.concatenate(owns, axis=1).astype(jnp.bfloat16)
     stacked = stacked_rows(grad).astype(jnp.bfloat16)
-    cube_ref[...] = jnp.zeros_like(cube_ref)
     for tap in range(9):
         tap_x, tap_y = tap // 3, tap % 3
         weight = kernel_ref[tap * 3 * channels : (tap + 1) * 3 * channels, :]
@@ -210,10 +268,9 @@
                     cube_ref[
                         (x + tap_x) * 6 + y + tap_y, :, z * channels : (z + 3) * channels
                     ] += part[row : row + bricks]
-    table_rows = table_ref.shape[0]
     slots = lax.broadcasted_iota(jnp.int32, (table_rows, 2 * bricks), 0)
     chooser = [
-        onehot(slots, jnp.broadcast_to(rows_ref[offset : offset + 1, :], slots.shape))
+        onehot(slots, jnp.broadcast_to(turned[offset : offset + 1, :], slots.shape))
         for offset in range(27)
     ]
     for xy in range(16):
@@ -245,9 +302,6 @@
         table_ref[:, start : start + channels] = total[:, :channels] + low
         table_ref[:, start + channels : start + 3 * channels] = total[:, channels : 3 * channels]
         table_ref[:, start + 3 * channels : start + wide] = total[:, 3 * channels :] + high
-    pick_rows = pick_ref.shape[0]
-    lanes = lax.broadcasted_iota(jnp.int32, (pick_rows, bricks), 1)
-    picker = onehot(lanes, jnp.broadcast_to(pick_ref[...], lanes.shape))
     for xy in range(16):
         span = slice(xy * wide, (xy + 1) * wide)
         sent = table_ref[:pick_rows, span] + jnp.dot(
@@ -263,8 +317,13 @@
     table_rows = table_ref.shape[0]
     channels = weight_ref.shape[1]
     wide = 4 * channels
-    lanes = lax.broadcasted_iota(jnp.int32, (27 * bricks, table_rows), 1)
-    chooser = onehot(lanes, jnp.broadcast_to(rows_ref[...], lanes.shape), jnp.float32)
+    lanes = lax.broadcasted_iota(jnp.int32, (bricks, table_rows), 1)
+    chooser = [
+        onehot(
+            lanes, jnp.broadcast_to(rows_ref[:, offset : offset + 1], lanes.shape), jnp.float32
+        )
+        for offset in range(27)
+    ]
     for xy in range(16):
         places = [
             (pos_x, pos_y)
@@ -277,7 +336,7 @@
             rows = []
             for pos_x, pos_y in places:
                 offset = 9 * SOURCES[pos_x][0] + 3 * SOURCES[pos_y][0] + side
-                rows.append(chooser[offset * bricks : (offset + 1) * bricks])
+                rows.append(chooser[offset])
             rows = rows[0] if len(rows) == 1 else jnp.concatenate(rows, axis=0)
             return jnp.dot(
                 rows.astype(jnp.bfloat16),
@@ -344,8 +403,7 @@
             preferred_element_type=jnp.float32,
         )
         total = part if total is None else total + part
-    owners = lax.broadcasted_iota(jnp.int32, (bricks, table_ref.shape[0]), 0)
-    backer = onehot(owners, jnp.broadcast_to(back_ref[...], owners.shape))
+    backer = back_ref[...]
     factor = jnp.broadcast_to(
         scan_ref[0].astype(jnp.float32) * scans / total_ref[0:1, :], (bricks, channels)
     )
@@ -389,50 +447,46 @@
     scan_count = lax.axis_size("x")
     steps = bit_axes({axis: lax.axis_size(axis) for axis in SPACE})
     levels = len(steps)
-    device = lax.axis_index(SPACE)
-    send_table = send_lists[0, 0]
-    peer_cap = send_table.shape[0] // nspace
+    peer_cap = send_lists.shape[2] // nspace
     assert peer_cap == 2 and bricks == 8
     send_rows = -(-4 * levels // 8) * 8
     table_rows = send_rows + bricks
     width = 64 * channels
-    mask_float = occupancy[0].reshape(bricks, 64).astype(jnp.float32)
-    kind, level_of, within = halo_place(brick_pairs[0].T, device, bricks, nspace, peer_cap, levels)
-    pair_table = brick_pairs[0].T
-    forward_rows = jnp.where(
-        kind == 0, send_rows + pair_table, jnp.where(kind == 1, 4 * level_of + within, -1)
-    )
-    backward_rows = jnp.where(kind == 1, forward_rows + peer_cap, forward_rows)
-    backward_rows = jnp.concatenate([backward_rows, backward_rows], axis=1)
-    forward_rows = forward_rows.reshape(27 * bricks, 1)
-    partners = jnp.bitwise_xor(device, jnp.left_shift(1, jnp.arange(levels, dtype=jnp.int32)))
-    entries = partners[:, None] * peer_cap + jnp.arange(peer_cap, dtype=jnp.int32)[None, :]
-    chosen = jnp.take(send_table, entries.reshape(-1)).reshape(levels, peer_cap)
-    nothing = jnp.full((levels, peer_cap), -1, jnp.int32)
-    pick_rows = jnp.pad(
-        jnp.concatenate([chosen, nothing], axis=1).reshape(-1),
-        (0, send_rows - 4 * levels),
-        constant_values=-1,
-    ).reshape(send_rows, 1)
-    back_rows = jnp.pad(
-        jnp.concatenate([nothing, chosen], axis=1).reshape(-1),
-        (0, table_rows - 4 * levels),
-        constant_values=-1,
-    ).reshape(1, table_rows)
     macs = own_rows * 27 * channels * channels
     cube = (36, bricks, 6 * channels)
     rowed = jax.ShapeDtypeStruct((bricks, width), jnp.bfloat16)
     plain = jax.ShapeDtypeStruct((own_rows, channels), jnp.bfloat16)
     natural = pltpu.VMEM((2, own_rows, channels), jnp.float32)
-    *sends, own_grad, masked, grad_in = local_call(
-        functools.partial(backward_kernel, levels),
+    *sends, own_grad, masked, grad_in, mask, forward_rows, backer = local_call(
+        functools.partial(backward_kernel, levels, peer_cap),
         [jax.ShapeDtypeStruct((4, width), jnp.bfloat16)] * levels
-        + [jax.ShapeDtypeStruct((bricks, width), jnp.float32), rowed, rowed],
-        [pltpu.VMEM(cube, jnp.float32), pltpu.VMEM((table_rows, width), jnp.float32), natural],
+        + [
+            jax.ShapeDtypeStruct((bricks, width), jnp.float32),
+            rowed,
+            rowed,
+            jax.ShapeDtypeStruct((bricks, 64), jnp.float32),
+            jax.ShapeDtypeStruct((bricks, 27), jnp.int32),
+            jax.ShapeDtypeStruct((bricks, table_rows), jnp.bfloat16),
+        ],
+        [
+            pltpu.VMEM(cube, jnp.float32),
+            pltpu.VMEM((table_rows, width), jnp.float32),
+            natural,
+            pltpu.VMEM((own_rows, channels), jnp.bfloat16),
+            pltpu.VMEM((own_rows, channels), jnp.bfloat16),
+            pltpu.VMEM(kernel.shape, jnp.bfloat16),
+            pltpu.VMEM((1, own_rows), jnp.int32),
+            pltpu.VMEM((bricks, 27), jnp.int32),
+            pltpu.SMEM((1, send_lists.shape[2]), jnp.int32),
+            pltpu.SemaphoreType.DMA((6,)),
+        ],
         2 * macs,
         4 * 2**20,
-    )(features[0], cotangent[0], mask_float, kernel, backward_rows, pick_rows)
-    came = [swapped(sends[level], steps[level]) for level in range(levels)]
+        [pl.BlockSpec(memory_space=pl.ANY)] * 6,
+    )(features[0], cotangent[0], kernel, occupancy, brick_pairs[0], send_lists[0])
+    came = [None] * levels
+    for level in range(levels):
+        came[level] = swapped(sends[level], steps[level])
     blank = jnp.zeros((send_rows - 4 * levels, width), jnp.bfloat16)
     table = jnp.concatenate(came + [blank, masked], axis=0)
     near_count = lax.axis_size("core") * lax.axis_size("x")
@@ -459,7 +513,7 @@
         2 * macs,
         4 * 2**20,
         [whole] * 7 + [scalar, whole],
-    )(cubes, kernel, table, masked, own_grad, back_rows, mask_float, scan_weight, weight_total)
+    )(cubes, kernel, table, masked, own_grad, backer, mask, scan_weight, weight_total)
     return (output[None], grad_features[None], kernel_grad)
 
 

time: 128 us -> 128 us (level)
    unnamed x15 -> x18, local copies, waits for them, and re-layouts: 5.4 us -> 6.66 us
where the time goes in v4:
time: 128 us
  blocking collectives  53.8 us (42%)
  starting transfers between devices  40.9 us (32%)
  waiting for transfers between devices  14.2 us (11%)
  Pallas kernels  10.3 us (8%)
  local copies, waits for them, and re-layouts  7.03 us (5%)
  between operations  1.46 us (1%)
    all_to_all x4, blocking collectives, exchanged(): return lax.all_to_all(parts, axes, 0, 0, tiled=True)  53.8 us
    ppermute x7, starting transfers between devices, swapped(): return lax.ppermute(value, axis, pairs)  33.3 us
    all_to_all x1, waiting for transfers between devices, exchanged(): return lax.all_to_all(parts, axes, 0, 0, tiled=True)  10.6 us
    all_to_all x1, starting transfers between devices, exchanged(): return lax.all_to_all(parts, axes, 0, 0, tiled=True)  7.57 us
    unnamed x18, local copies, waits for them, and re-layouts  6.66 us
    pallas_call x1, Pallas kernels, on_device(): local_call(functools.partial(backward_kernel, levels, peer_cap), [jax.Sha...  3.7 us
    ppermute x7, waiting for transfers between devices, swapped(): return lax.ppermute(value, axis, pairs)  3.58 us
  transfers between devices with their start and end apart: 8, of which 2 were waited for; matrix products, arithmetic and copies ran while one was open for 0% of the time, Pallas kernels for 2%

profile of v4, /device:TPU:1, one launch (start us, length us, event | category | flops | bytes accessed | tf_op | source)
XLA Modules:
  0.0 127.6 jit_solution(377050351004034717)
XLA Ops:
  0.6 1.2 copy-done
  1.8 0.9 copy-done.4
  2.7 0.9 copy-done.5
  5.7 3.7 %shard_map.94 = (bf16[4,8192]{1,0:T(4,128)(2,1)S(1)}, bf16[4,8192]{1,0:T(4,128)(2,1)S(1)}, bf16[4,8192]{1,0:T(4,128)(2,1)S(1)}, bf16[4,8192]{1,0:T(4,128)(2,1)S(...) custom-call(bf16[512,128]{1,0:T(8,128)(2,1)S(1)} %bitcast.6, ...), custom_call_target="tpu_custom_call" | custom-call | flops 452984832 | bytes 4194304 | tf_op jit(solution)/shard_map/pallas_call | solution.py:460
  9.4 0.7 copy-done.2
  10.1 8.7 %collective-permute-start = (bf16[4,8192]{1,0:T(4,128)(2,1)S(1)}, bf16[4,8192]{1,0:T(4,128)(2,1)S(1)}, u32[]{:S(2)}, u32[]{:S(2)}) collective-permute-start(bf16[4,8192]{1,0:T(4,128)(2,1)S(1)} %get-tuple-element.22), channel_id=1, source_target_pairs={{0,4},{4,0},{1,5},{5,1},{2,6},{6,2},{3,7},{7,3},{8,12},{12,8},{9,1... | collective-permute-start | bytes 196616 | tf_op jit(solution)/shard_map/ppermute | solution.py:27
  18.8 1.9 %collective-permute-start.1 = (bf16[4,8192]{1,0:T(4,128)(2,1)S(1)}, bf16[4,8192]{1,0:T(4,128)(2,1)S(1)}, u32[]{:S(2)}, u32[]{:S(2)}) collective-permute-start(bf16[4,8192]{1,0:T(4,128)(2,1)S(1)} %get-tuple-element.23), channel_id=1, source_target_pairs={{0,8},{8,0},{16,24},{24,16},{32,40},{40,32},{48,56},{56,48},{1,9},... | collective-permute-start | bytes 196616 | tf_op jit(solution)/shard_map/ppermute | solution.py:27
  20.7 2.5 %collective-permute-start.2 = (bf16[4,8192]{1,0:T(4,128)(2,1)S(1)}, bf16[4,8192]{1,0:T(4,128)(2,1)S(1)}, u32[]{:S(2)}, u32[]{:S(2)}) collective-permute-start(bf16[4,8192]{1,0:T(4,128)(2,1)S(1)} %get-tuple-element.24), channel_id=1, source_target_pairs={{0,16},{8,24},{16,0},{24,8},{32,48},{40,56},{48,32},{56,40},{1,17}... | collective-permute-start | bytes 196616 | tf_op jit(solution)/shard_map/ppermute | solution.py:27
  23.3 7.9 %collective-permute-start.3 = (bf16[4,8192]{1,0:T(4,128)(2,1)S(1)}, bf16[4,8192]{1,0:T(4,128)(2,1)S(1)}, u32[]{:S(2)}, u32[]{:S(2)}) collective-permute-start(bf16[4,8192]{1,0:T(4,128)(2,1)S(1)} %get-tuple-element.25), channel_id=1, source_target_pairs={{0,32},{8,40},{16,48},{24,56},{32,0},{40,8},{48,16},{56,24},{1,33}... | collective-permute-start | bytes 196616 | tf_op jit(solution)/shard_map/ppermute | solution.py:27
  31.2 3.2 %collective-permute-start.4 = (bf16[4,8192]{1,0:T(4,128)(2,1)S(1)}, bf16[4,8192]{1,0:T(4,128)(2,1)S(1)}, u32[]{:S(2)}, u32[]{:S(2)}) collective-permute-start(bf16[4,8192]{1,0:T(4,128)(2,1)S(1)} %get-tuple-element.26), channel_id=1, source_target_pairs={{0,64},{64,0},{128,192},{192,128},{256,320},{320,256},{384,448},{4... | collective-permute-start | bytes 196616 | tf_op jit(solution)/shard_map/ppermute | solution.py:27
  34.5 4.2 %collective-permute-start.5 = (bf16[4,8192]{1,0:T(4,128)(2,1)S(1)}, bf16[4,8192]{1,0:T(4,128)(2,1)S(1)}, u32[]{:S(2)}, u32[]{:S(2)}) collective-permute-start(bf16[4,8192]{1,0:T(4,128)(2,1)S(1)} %get-tuple-element.27), channel_id=1, source_target_pairs={{0,128},{64,192},{128,0},{192,64},{256,384},{320,448},{384,256},{4... | collective-permute-start | bytes 196616 | tf_op jit(solution)/shard_map/ppermute | solution.py:27
  38.7 4.8 %collective-permute-start.6 = (bf16[4,8192]{1,0:T(4,128)(2,1)S(1)}, bf16[4,8192]{1,0:T(4,128)(2,1)S(1)}, u32[]{:S(2)}, u32[]{:S(2)}) collective-permute-start(bf16[4,8192]{1,0:T(4,128)(2,1)S(1)} %get-tuple-element.28), channel_id=1, source_target_pairs={{0,256},{64,320},{128,384},{192,448},{256,0},{320,64},{384,128},{4... | collective-permute-start | bytes 196616 | tf_op jit(solution)/shard_map/ppermute | solution.py:27
  44.2 3.6 %collective-permute-done.6 = bf16[4,8192]{1,0:T(4,128)(2,1)S(1)} collective-permute-done((bf16[4,8192]{1,0:T(4,128)(2,1)S(1)}, bf16[4,8192]{1,0:T(4,128)(2,1)S(1)}, u32[]{:S(2)}, u32[]{:S(2)}) %collective-permute-start.6) | collective-permute-done | bytes 65568 | tf_op jit(solution)/shard_map/ppermute | solution.py:27
  48.1 1.4 %shard_map.95 = (s16[8,448,128]{2,1,0:T(8,128)(2,1)S(1)}, f32[36,8,768]{2,1,0:T(8,128)S(1)}) custom-call(bf16[40,8192]{1,0:T(8,128)(2,1)S(1)} %concatenate.3.table_ref, bf16[8,8192]{1,0:T(8,128)(2,1)S(1)} %get-tuple-element.30.grad_ref, s32[8,27]{1,0:T(8,128)S(1)} %get-tuple-element.31.rows_ref, s32[1]{0:T(128)S(6)} %copy.10.scan_ref), custom_call_target="tpu_custom_call" | custom-call | flops 452984832 | bytes 4194304 | tf_op jit(solution)/shard_map/pallas_call | solution.py:496
  49.6 20.5 %all_to_all.25.coded_ref = s16[8,448,128]{2,1,0:T(8,128)(2,1)S(1)} all-to-all(s16[8,448,128]{2,1,0:T(8,128)(2,1)S(1)} %get-tuple-element.36), channel_id=1, replica_groups=mesh['y'=8,'z'=8,'core'=2,'x'=4] {'core','x'}, dimensions={0} | all-to-all | bytes 1835008 | tf_op jit(solution)/shard_map/all_to_all | solution.py:94
  70.5 10.7 %all_to_all.26.coded_ref = s16[8,64,128]{2,1,0:T(8,128)(2,1)S(1)} all-to-all(s16[8,64,128]{2,1,0:T(8,128)(2,1)S(1)} %get-tuple-element.40), channel_id=1, replica_groups=mesh['y'=8,'z'=8,'core'=2,'x'=4] {'z'}, dimensions={0} | all-to-all | bytes 262144 | tf_op jit(solution)/shard_map/all_to_all | solution.py:94
  81.2 12.1 %all_to_all.27.coded_ref = s16[8,64,128]{2,1,0:T(8,128)(2,1)S(1)} all-to-all(s16[8,64,128]{2,1,0:T(8,128)(2,1)S(1)} %shard_map.98), channel_id=1, replica_groups=mesh['y'=8,'z'=8,'core'=2,'x'=4] {'y'}, dimensions={0} | all-to-all | bytes 262144 | tf_op jit(solution)/shard_map/all_to_all | solution.py:94
  93.4 10.5 %all_to_all.28.coded_ref = s16[8,64,128]{2,1,0:T(8,128)(2,1)S(1)} all-to-all(s16[8,64,128]{2,1,0:T(8,128)(2,1)S(1)} %shard_map.99), channel_id=1, replica_groups=mesh['y'=8,'z'=8,'core'=2,'x'=4] {'z'}, dimensions={0} | all-to-all | bytes 262144 | tf_op jit(solution)/shard_map/all_to_all | solution.py:94
  103.9 1.1 shard_map.100
  105.0 7.6 %all-to-all-start.4 = ((s16[8,448,128]{2,1,0:T(8,128)(2,1)}), s16[8,448,128]{2,1,0:T(8,128)(2,1)S(1)}, u32[]{:S(2)}, u32[]{:S(2)}) async-start(s16[8,448,128]{2,1,0:T(8,128)(2,1)} %shard_map.100), calls=%async_computation.4 | async-start | bytes 1835008 | tf_op jit(solution)/shard_map/all_to_all | solution.py:94
  112.6 0.9 copy-done.3
  113.6 2.0 %shard_map.97 = (bf16[512,128]{1,0:T(8,128)(2,1)}, bf16[512,128]{1,0:T(8,128)(2,1)}) custom-call(f32[36,8,768]{2,1,0:T(8,128)S(1)} %get-tuple-element.32.cube_ref, bf16[3456,128]{1,0:T(8,128)(2,1)S(1)} %copy-done.1, bf16[40,8192]{1,0:T(8,128)(2,1)S(1)} %concatenate.3.table_ref, bf16[8,8192]{1,0:T(8,128)(2,1)S(1)} %get-tuple-element.29.own_ref, ...), custom_call_target="tpu_custom_call" | custom-call | flops 452984832 | bytes 4194304 | tf_op jit(solution)/shard_map/pallas_call | solution.py:509
  115.6 10.6 %all-to-all-done.4.coded_ref = s16[8,448,128]{2,1,0:T(8,128)(2,1)S(1)} async-done(((s16[8,448,128]{2,1,0:T(8,128)(2,1)}), s16[8,448,128]{2,1,0:T(8,128)(2,1)S(1)}, u32[]{:S(2)}, u32[]{:S(2)}) %all-to-all-start.4) | async-done | bytes 917536 | tf_op jit(solution)/shard_map/all_to_all | solution.py:94
  126.2 1.4 %shard_map.101 = f32[3456,128]{1,0:T(8,128)} custom-call(s16[8,448,128]{2,1,0:T(8,128)(2,1)S(1)} %all-to-all-done.4.coded_ref, f32[8,128]{1,0:T(8,128)S(1)} %get-tuple-element.37.total_ref), custom_call_target="tpu_custom_call" | custom-call | flops 1769472 | bytes 2654208 | tf_op jit(solution)/shard_map/pallas_call | solution.py:123
  (24 shorter events, 3.0 us)
Async XLA Ops:
  0.6 1.2 copy-start
  1.8 0.9 copy-start.4
  2.7 0.9 copy-start.5
  3.6 0.7 copy-start.6
  4.3 0.7 copy-start.7
  5.0 0.7 copy-start.8
  9.4 0.7 copy-start.2
  10.1 24.4 %collective-permute-start = (bf16[4,8192]{1,0:T(4,128)(2,1)S(1)}, bf16[4,8192]{1,0:T(4,128)(2,1)S(1)}, u32[]{:S(2)}, u32[]{:S(2)}) collective-permute-start(bf16[4,8192]{1,0:T(4,128)(2,1)S(1)} %get-tuple-element.22), channel_id=1, source_target_pairs={{0,4},{4,0},{1,5},{5,1},{2,6},{6,2},{3,7},{7,3},{8,12},{12,8},{9,1... | collective-permute-start | bytes 196616 | tf_op jit(solution)/shard_map/ppermute | solution.py:27
  18.8 19.9 %collective-permute-start.1 = (bf16[4,8192]{1,0:T(4,128)(2,1)S(1)}, bf16[4,8192]{1,0:T(4,128)(2,1)S(1)}, u32[]{:S(2)}, u32[]{:S(2)}) collective-permute-start(bf16[4,8192]{1,0:T(4,128)(2,1)S(1)} %get-tuple-element.23), channel_id=1, source_target_pairs={{0,8},{8,0},{16,24},{24,16},{32,40},{40,32},{48,56},{56,48},{1,9},... | collective-permute-start | bytes 196616 | tf_op jit(solution)/shard_map/ppermute | solution.py:27
  20.7 23.4 %collective-permute-start.2 = (bf16[4,8192]{1,0:T(4,128)(2,1)S(1)}, bf16[4,8192]{1,0:T(4,128)(2,1)S(1)}, u32[]{:S(2)}, u32[]{:S(2)}) collective-permute-start(bf16[4,8192]{1,0:T(4,128)(2,1)S(1)} %get-tuple-element.24), channel_id=1, source_target_pairs={{0,16},{8,24},{16,0},{24,8},{32,48},{40,56},{48,32},{56,40},{1,17}... | collective-permute-start | bytes 196616 | tf_op jit(solution)/shard_map/ppermute | solution.py:27
  23.3 20.8 %collective-permute-start.3 = (bf16[4,8192]{1,0:T(4,128)(2,1)S(1)}, bf16[4,8192]{1,0:T(4,128)(2,1)S(1)}, u32[]{:S(2)}, u32[]{:S(2)}) collective-permute-start(bf16[4,8192]{1,0:T(4,128)(2,1)S(1)} %get-tuple-element.25), channel_id=1, source_target_pairs={{0,32},{8,40},{16,48},{24,56},{32,0},{40,8},{48,16},{56,24},{1,33}... | collective-permute-start | bytes 196616 | tf_op jit(solution)/shard_map/ppermute | solution.py:27
  31.2 12.9 %collective-permute-start.4 = (bf16[4,8192]{1,0:T(4,128)(2,1)S(1)}, bf16[4,8192]{1,0:T(4,128)(2,1)S(1)}, u32[]{:S(2)}, u32[]{:S(2)}) collective-permute-start(bf16[4,8192]{1,0:T(4,128)(2,1)S(1)} %get-tuple-element.26), channel_id=1, source_target_pairs={{0,64},{64,0},{128,192},{192,128},{256,320},{320,256},{384,448},{4... | collective-permute-start | bytes 196616 | tf_op jit(solution)/shard_map/ppermute | solution.py:27
  34.5 9.7 %collective-permute-start.5 = (bf16[4,8192]{1,0:T(4,128)(2,1)S(1)}, bf16[4,8192]{1,0:T(4,128)(2,1)S(1)}, u32[]{:S(2)}, u32[]{:S(2)}) collective-permute-start(bf16[4,8192]{1,0:T(4,128)(2,1)S(1)} %get-tuple-element.27), channel_id=1, source_target_pairs={{0,128},{64,192},{128,0},{192,64},{256,384},{320,448},{384,256},{4... | collective-permute-start | bytes 196616 | tf_op jit(solution)/shard_map/ppermute | solution.py:27
  38.7 9.0 %collective-permute-start.6 = (bf16[4,8192]{1,0:T(4,128)(2,1)S(1)}, bf16[4,8192]{1,0:T(4,128)(2,1)S(1)}, u32[]{:S(2)}, u32[]{:S(2)}) collective-permute-start(bf16[4,8192]{1,0:T(4,128)(2,1)S(1)} %get-tuple-element.28), channel_id=1, source_target_pairs={{0,256},{64,320},{128,384},{192,448},{256,0},{320,64},{384,128},{4... | collective-permute-start | bytes 196616 | tf_op jit(solution)/shard_map/ppermute | solution.py:27
  93.3 19.3 %copy-start.1 = (bf16[3456,128]{1,0:T(8,128)(2,1)S(1)}, bf16[3456,128]{1,0:T(8,128)(2,1)}, u32[]{:S(2)}) copy-start(bf16[3456,128]{1,0:T(8,128)(2,1)} %kernel_ref.1) | copy-start | bytes 2654212
  105.0 21.1 %all-to-all-start.4 = ((s16[8,448,128]{2,1,0:T(8,128)(2,1)}), s16[8,448,128]{2,1,0:T(8,128)(2,1)S(1)}, u32[]{:S(2)}, u32[]{:S(2)}) async-start(s16[8,448,128]{2,1,0:T(8,128)(2,1)} %shard_map.100), calls=%async_computation.4 | async-start | bytes 1835008 | tf_op jit(solution)/shard_map/all_to_all | solution.py:94
  112.6 1.0 copy-start.3
